TPU v7x, 32 devices: a whole 2x2x4 slice. The times are simulated.
32 devices in a mesh: wide: 8 (over y, x, core), group: 4 (over z).
Axes of the slice: x: 2, y: 2, z: 4, core: 2. Of those that a mesh axis runs over, the one named last changes fastest.
Arguments:
- inputs: bfloat16 [32, 128, 576], P(('wide', 'group')), may hold values from -6 to 6
- segments: int32 [32, 128], P(('wide', 'group')), may hold values from 0 to 5, never falling along the last dimension, each value on 1 to 64 neighbouring positions
- cotangent: bfloat16 [32, 128, 576], P(('wide', 'group')), may hold values from -6 to 6
- params: float32 [3540096], P('group')
- moment_one: float32 [3540096], P('group')
- moment_two: float32 [3540096], P('group')
Outputs:
- outputs: bfloat16 [32, 128, 576], P(('wide', 'group'))
- d_inputs: bfloat16 [32, 128, 576], P(('wide', 'group'))
- grads: float32 [3540096], P('group')
- new_params: float32 [3540096], P('group')
- new_moment_one: float32 [3540096], P('group')
- new_moment_two: float32 [3540096], P('group')
All inputs are finite; a program needn't handle non-finite values.
Results may differ from a plain program's by a relative error of at most 0.023.
Values may be sent and summed in bfloat16 or wider, within the bound.
A program may use at most 128 MiB of HBM per device.

v0:
```python
import math

import jax
import jax.numpy as jnp
from jax import lax
from jax.sharding import PartitionSpec as P

MODEL_WIDTH = 576
QUERY_HEADS = 9
KEY_VALUE_HEADS = 3
HEAD_SIZE = 64
FF = 1536


norm_eps = 1e-05
theta_base = 10000.0
masked_value = -1e30
beta_one = 0.9
beta_two = 0.95
bias_one = 0.19
bias_two = 0.0975
learn_rate = 0.03
decay_rate = 0.1
adam_eps = 1e-08
max_norm = 1.0


def contract(pattern, left_op, right_op):
    return jnp.einsum(pattern, left_op, right_op, preferred_element_type=jnp.float32)


def inner_rows(left_op, right_op):
    return lax.dot_general(
        left_op, right_op, (((0,), (0,)), ((), ())), preferred_element_type=jnp.float32
    )


def outer_column_count(left_op, right_op):
    return lax.dot_general(
        left_op, right_op, (((1,), (1,)), ((), ())), preferred_element_type=jnp.float32
    )


def unpack(flat):
    query_key_value_width = (QUERY_HEADS + 2 * KEY_VALUE_HEADS) * HEAD_SIZE
    shapes = [
        (MODEL_WIDTH, query_key_value_width),
        (QUERY_HEADS * HEAD_SIZE, MODEL_WIDTH),
        (MODEL_WIDTH, 2 * FF),
        (FF, MODEL_WIDTH),
        (MODEL_WIDTH,),
        (MODEL_WIDTH,),
    ]
    pieces = []
    offset = 0
    for piece_shape in shapes:
        extent = math.prod(piece_shape)
        pieces.append(flat[offset : offset + extent].reshape(piece_shape))
        offset += extent
    return pieces


def positions_of(segment_row):
    index_row = jnp.arange(segment_row.shape[0], dtype=jnp.int32)
    previous = jnp.concatenate([segment_row[:1] - 1, segment_row[:-1]])
    starts = jnp.where(segment_row != previous, index_row, jnp.zeros_like(index_row))
    return index_row - lax.cummax(starts, axis=0)


def rope_tables(positions):
    half_size = HEAD_SIZE // 2
    freqs = theta_base ** (-2.0 * jnp.arange(half_size, dtype=jnp.float32) / HEAD_SIZE)
    angles = positions.astype(jnp.float32)[:, None] * freqs[None, :]
    return (jnp.cos(angles)[:, None, :], jnp.sin(angles)[:, None, :])


def apply_rotation(vectors, cosine_lookup, sine_lookup):
    half_size = HEAD_SIZE // 2
    first_half = vectors[..., :half_size]
    second_half = vectors[..., half_size:]
    return jnp.concatenate(
        [
            first_half * cosine_lookup - second_half * sine_lookup,
            second_half * cosine_lookup + first_half * sine_lookup,
        ],
        axis=-1,
    )


def unrotate(vectors, cosine_lookup, sine_lookup):
    half_size = HEAD_SIZE // 2
    first_half = vectors[..., :half_size]
    second_half = vectors[..., half_size:]
    return jnp.concatenate(
        [
            first_half * cosine_lookup + second_half * sine_lookup,
            second_half * cosine_lookup - first_half * sine_lookup,
        ],
        axis=-1,
    )


def norm_back(d_hidden, normed, inverse, gain):
    d_normed = d_hidden * gain
    return inverse * (d_normed - normed * jnp.mean(d_normed * normed, axis=-1, keepdims=True))


def layer_row(inputs, segment_row, cotangent, weights):
    query_key_value_weight, output_weight, w_gateup, w_down, gain_attn, gain_ffn = weights
    sequence_length = inputs.shape[0]
    repeat_count = QUERY_HEADS // KEY_VALUE_HEADS
    scale_factor = HEAD_SIZE ** (-0.5)
    gain_one = gain_attn.astype(jnp.float32)
    gain_two = gain_ffn.astype(jnp.float32)
    resid_in = inputs.astype(jnp.float32)
    inv_attn = lax.rsqrt(jnp.mean(resid_in * resid_in, axis=-1, keepdims=True) + norm_eps)
    normed_attn = resid_in * inv_attn
    hidden_attn = (normed_attn * gain_one).astype(jnp.bfloat16)
    projected_output = jnp.dot(
        hidden_attn, query_key_value_weight, preferred_element_type=jnp.float32
    )
    cosine_lookup, sine_lookup = rope_tables(positions_of(segment_row))
    query_rows = projected_output[:, : QUERY_HEADS * HEAD_SIZE].reshape(
        sequence_length, QUERY_HEADS, HEAD_SIZE
    )
    key_matrix = projected_output[
        :, QUERY_HEADS * HEAD_SIZE : (QUERY_HEADS + KEY_VALUE_HEADS) * HEAD_SIZE
    ].reshape(sequence_length, KEY_VALUE_HEADS, HEAD_SIZE)
    query_rows_rotated = (
        apply_rotation(query_rows, cosine_lookup, sine_lookup)
        .astype(jnp.bfloat16)
        .reshape(sequence_length, KEY_VALUE_HEADS, repeat_count, HEAD_SIZE)
    )
    keys_rot = apply_rotation(key_matrix, cosine_lookup, sine_lookup).astype(jnp.bfloat16)
    value_rows = (
        projected_output[:, (QUERY_HEADS + KEY_VALUE_HEADS) * HEAD_SIZE :]
        .reshape(sequence_length, KEY_VALUE_HEADS, HEAD_SIZE)
        .astype(jnp.bfloat16)
    )
    index_row = jnp.arange(sequence_length)
    allowed = (segment_row[:, None] == segment_row[None, :]) & (
        index_row[:, None] >= index_row[None, :]
    )
    scores = contract("qgrd,kgd->grqk", query_rows_rotated, keys_rot) * scale_factor
    scores = jnp.where(allowed, scores, masked_value)
    peak = jnp.max(scores, axis=-1, keepdims=True)
    log_total = peak + jnp.log(jnp.sum(jnp.exp(scores - peak), axis=-1, keepdims=True))
    probs_b = jnp.exp(scores - log_total).astype(jnp.bfloat16)
    attended = (
        contract("grqk,kgd->qgrd", probs_b, value_rows)
        .astype(jnp.bfloat16)
        .reshape(sequence_length, QUERY_HEADS * HEAD_SIZE)
    )
    mid = resid_in + jnp.dot(attended, output_weight, preferred_element_type=jnp.float32)
    inv_ffn = lax.rsqrt(jnp.mean(mid * mid, axis=-1, keepdims=True) + norm_eps)
    normed_ffn = mid * inv_ffn
    hidden_ffn = (normed_ffn * gain_two).astype(jnp.bfloat16)
    gate_up = jnp.dot(hidden_ffn, w_gateup, preferred_element_type=jnp.float32)
    gate_pre = gate_up[:, :FF]
    upper = gate_up[:, FF:]
    sigmoid_gate = jax.nn.sigmoid(gate_pre)
    activation = (gate_pre * sigmoid_gate * upper).astype(jnp.bfloat16)
    outputs = (mid + jnp.dot(activation, w_down, preferred_element_type=jnp.float32)).astype(
        jnp.bfloat16
    )
    grad_down = inner_rows(activation, cotangent)
    d_act = outer_column_count(cotangent, w_down)
    d_gate = d_act * upper * sigmoid_gate * (1.0 + gate_pre * (1.0 - sigmoid_gate))
    d_upper = d_act * gate_pre * sigmoid_gate
    d_gate_up = jnp.concatenate([d_gate, d_upper], axis=-1).astype(jnp.bfloat16)
    grad_gateup = inner_rows(hidden_ffn, d_gate_up)
    d_hidden_ffn = outer_column_count(d_gate_up, w_gateup)
    grad_gain_ffn = jnp.sum(d_hidden_ffn * normed_ffn, axis=0)
    d_mid = cotangent.astype(jnp.float32) + norm_back(d_hidden_ffn, normed_ffn, inv_ffn, gain_two)
    grad_middle_batch = d_mid.astype(jnp.bfloat16)
    grad_out = inner_rows(attended, grad_middle_batch)
    grad_attended_rows = (
        outer_column_count(grad_middle_batch, output_weight)
        .astype(jnp.bfloat16)
        .reshape(sequence_length, KEY_VALUE_HEADS, repeat_count, HEAD_SIZE)
    )
    recomputed = contract("qgrd,kgd->grqk", query_rows_rotated, keys_rot) * scale_factor
    probs = jnp.exp(jnp.where(allowed, recomputed, masked_value) - log_total)
    d_probs = contract("qgrd,kgd->grqk", grad_attended_rows, value_rows)
    row_total = jnp.sum(probs * d_probs, axis=-1, keepdims=True)
    d_scores = (probs * (d_probs - row_total) * scale_factor).astype(jnp.bfloat16)
    grad_query_rows = contract("grqk,kgd->qgrd", d_scores, keys_rot).reshape(
        sequence_length, QUERY_HEADS, HEAD_SIZE
    )
    grad_key_rows = contract("grqk,qgrd->kgd", d_scores, query_rows_rotated)
    grad_value_rows = contract("grqk,qgrd->kgd", probs_b, grad_attended_rows)
    grad_query_rows = unrotate(grad_query_rows, cosine_lookup, sine_lookup)
    grad_key_rows = unrotate(grad_key_rows, cosine_lookup, sine_lookup)
    grad_projected_rows = jnp.concatenate(
        [
            grad_query_rows.reshape(sequence_length, QUERY_HEADS * HEAD_SIZE),
            grad_key_rows.reshape(sequence_length, KEY_VALUE_HEADS * HEAD_SIZE),
            grad_value_rows.reshape(sequence_length, KEY_VALUE_HEADS * HEAD_SIZE),
        ],
        axis=-1,
    ).astype(jnp.bfloat16)
    grad_qkv = inner_rows(hidden_attn, grad_projected_rows)
    d_hidden_attn = outer_column_count(grad_projected_rows, query_key_value_weight)
    grad_gain_attn = jnp.sum(d_hidden_attn * normed_attn, axis=0)
    d_inputs = (d_mid + norm_back(d_hidden_attn, normed_attn, inv_attn, gain_one)).astype(
        jnp.bfloat16
    )
    flat_grads = jnp.concatenate(
        [
            grad_qkv.reshape(-1),
            grad_out.reshape(-1),
            grad_gateup.reshape(-1),
            grad_down.reshape(-1),
            grad_gain_attn,
            grad_gain_ffn,
        ]
    )
    return (outputs, d_inputs, flat_grads)


def adam_update(grads, clip_factor, params, moment_one, moment_two, decay_mask):
    clipped = grads * clip_factor
    new_moment_one = beta_one * moment_one + (1.0 - beta_one) * clipped
    new_moment_two = beta_two * moment_two + (1.0 - beta_two) * clipped * clipped
    step_size = new_moment_one / bias_one / (jnp.sqrt(new_moment_two / bias_two) + adam_eps)
    decay_term = jnp.where(decay_mask, decay_rate * params, jnp.zeros_like(params))
    new_params = params - learn_rate * (step_size + decay_term)
    return (new_params, new_moment_one, new_moment_two)


def on_device(inputs, segments, cotangent, params, moment_one, moment_two):
    working = lax.all_gather(params.astype(jnp.bfloat16), "group", axis=0, tiled=True)
    weights = unpack(working)
    outputs, d_inputs, local_grads = layer_row(inputs[0], segments[0], cotangent[0], weights)
    groups = lax.axis_size("group")
    wides = lax.axis_size("wide")
    share_len = params.shape[0]
    piece_len = -(-share_len // wides)
    shares = lax.psum_scatter(
        local_grads.astype(jnp.bfloat16), "group", scatter_dimension=0, tiled=True
    ).astype(jnp.float32)
    padded = jnp.pad(shares, (0, piece_len * wides - share_len)).reshape(wides, piece_len)
    owned_piece = lax.psum_scatter(
        padded.astype(jnp.bfloat16), "wide", scatter_dimension=0, tiled=True
    ).astype(jnp.float32)
    collected_share = lax.all_gather(
        owned_piece.astype(jnp.bfloat16), "wide", axis=0, tiled=True
    ).astype(owned_piece.dtype)
    summed = collected_share.reshape(-1)[:share_len]
    squares = lax.psum(jnp.sum(summed * summed), "group")
    clip_factor = jnp.minimum(jnp.float32(1.0), max_norm * lax.rsqrt(squares))
    flat_index = lax.axis_index("group") * share_len + jnp.arange(share_len, dtype=jnp.int32)
    decay_mask = flat_index < share_len * groups - 2 * MODEL_WIDTH
    new_params, new_moment_one, new_moment_two = adam_update(
        summed, clip_factor, params, moment_one, moment_two, decay_mask
    )
    return (outputs[None], d_inputs[None], summed, new_params, new_moment_one, new_moment_two)


def solution(mesh):
    return jax.shard_map(
        on_device,
        mesh=mesh,
        in_specs=(
            P(("wide", "group"), None, None),
            P(("wide", "group"), None),
            P(("wide", "group"), None, None),
            P("group"),
            P("group"),
            P("group"),
        ),
        out_specs=(
            P(("wide", "group"), None, None),
            P(("wide", "group"), None, None),
            P("group"),
            P("group"),
            P("group"),
            P("group"),
        ),
        check_vma=False,
    )
```

profile of v0, /device:TPU:0, one launch (start us, length us, event | category | flops | bytes accessed | tf_op | source)
XLA Modules:
  0.0 858.7 jit_solution(7309640272082544102)
XLA Ops:
  10.7 3.4 broadcast.120
  14.1 27.6 %dynamic-update-slice = bf16[3540096]{0:T(1024)(128)(2,1)} dynamic-update-slice(bf16[3540096]{0:T(1024)(128)(2,1)} %broadcast.120, bf16[885024]{0:T(1024)(128)(2,1)S(1)} %convert_element_type.89, u32[]{:T(128)} %bitcast.1) | dynamic-update-slice | bytes 3540100
  43.2 250.0 %all-reduce.7.cloned.1.call-done = bf16[3540096]{0:T(1024)(128)(2,1)} async-done(((bf16[3540096]{0:T(1024)(128)(2,1)}), bf16[3540096]{0:T(1024)(128)(2,1)}) %all-reduce.7.cloned.1.call-update) | async-done | bytes 7080208
  301.7 3.4 slice.114
  305.1 5.0 reshape.278
  310.1 2.8 slice.117
  312.9 4.3 reshape.279
  324.7 2.3 convolution_bitcast_fusion.3
  333.5 2.9 fusion.2
  338.0 2.2 reshape.285
  342.1 2.7 copy.34
  344.8 3.2 reshape.288
  348.0 3.0 copy.44
  351.1 87.1 %concatenate.55 = bf16[3540096]{0:T(1024)(128)(2,1)} concatenate(bf16[552960]{0:T(1024)(128)(2,1)} %reshape.285, bf16[331776]{0:T(1024)(128)(2,1)} %reshape.286, bf16[1769472]{0:T(1024)(128)(2,1)S(1)} %bitcast.128, bf16[884736]{0:T(1024)(128)(2,1)} %reshape.288, bf16[576]{0:T(1024)(128)(2,1)S(1)} %get-tuple-element.10, bf16[576]{0:T(1024)(128)(2,1)S(1)} %copy-done.51), dimensions={0} | concatenate | bytes 14160384 | tf_op jit(solution)/shard_map/concatenate | solution.py:208
  439.1 246.9 %all-reduce.9.cloned.1.call-done = bf16[3540096]{0:T(1024)(128)(2,1)} async-done(((bf16[3540096]{0:T(1024)(128)(2,1)}), bf16[3540096]{0:T(1024)(128)(2,1)}) %all-reduce.9.cloned.1.call-update) | async-done | bytes 7080208
  686.0 3.6 dynamic-slice.2
  689.6 5.0 convert_element_type.108
  695.4 58.3 %all-reduce.11.cloned.1.call-done = bf16[8,110628]{1,0:T(8,128)(2,1)} async-done(((bf16[8,110628]{1,0:T(8,128)(2,1)}), bf16[8,110628]{1,0:T(8,128)(2,1)}) %all-reduce.11.cloned.1.call-update) | async-done | bytes 1770064
  753.7 3.3 dynamic-slice_bitcast_fusion
  759.4 31.2 %all-gather.3.cloned.1.call-done = bf16[8,1,110628]{2,1,0:T(2,128)(2,1)} async-done(((bf16[1,1,110628]{2,1,0:T(2,128)(2,1)}), bf16[8,1,110628]{2,1,0:T(2,128)(2,1)}) %all-gather.3.cloned.1.call-update) | async-done | bytes 1770064 | tf_op jit(solution)/shard_map/all_gather | solution.py:246
  790.6 34.5 %multiply_reduce_fusion = (f32[]{:T(128)}, f32[8,110628]{1,0:T(8,128)}) fusion(bf16[8,1,110628]{2,1,0:T(2,128)(2,1)} %all-gather.3.cloned.1.call-done), kind=kLoop, calls=%fused_computation.4 | loop fusion | flops 2655071 | bytes 5310148 | tf_op jit(solution)/shard_map/reduce_sum | solution.py:250
  825.1 12.3 %psum.7 = f32[]{:T(128)} all-reduce(f32[]{:T(128)} %get-tuple-element.6), channel_id=1, replica_groups=mesh['wide'=8,'group'=4] {'group'}, use_global_device_ids=true, to_apply=%region_13.14 | all-reduce | flops 1 | bytes 8 | tf_op jit(solution)/shard_map/psum | solution.py:250
  838.1 5.8 reshape.289
  843.9 8.2 multiply_subtract_fusion
  (169 shorter events, 32.9 us)
Async XLA Ops:
  7.2 286.1 %all-reduce.7.cloned.1.call-start = ((), (), s32[]{:S(2)}) async-start(), calls=%async_computation | async-start | bytes 14163968
  41.7 644.3 %all-reduce.9.cloned.1.call-start = ((), (), s32[]{:S(2)}) async-start(), calls=%async_computation.2 | async-start | bytes 14163968
  43.0 254.9 %copy-start.49 = (f32[128]{0:T(128)}, f32[128]{0:T(128)S(1)}, u32[]{:S(2)}) copy-start(f32[128]{0:T(128)S(1)} %add_rsqrt_fusion.1) | copy-start | bytes 1540
  43.2 255.3 %copy-start.25 = (f32[128,32]{0,1:T(8,128)}, f32[128,32]{0,1:T(8,128)S(1)}, u32[]{:S(2)}) copy-start(f32[128,32]{0,1:T(8,128)S(1)} %get-tuple-element.29) | copy-start | bytes 49156
  322.9 6.2 copy-start.26
  323.0 7.0 copy-start.12
  323.0 7.0 copy-start.11
  323.1 7.0 copy-start.15
  323.1 7.0 copy-start.39
  327.0 6.4 copy-start.2
  327.0 6.4 copy-start.28
  327.0 6.5 copy-start.33
  333.5 6.8 copy-start.17
  333.5 6.8 copy-start.22
  438.2 315.5 %all-reduce.11.cloned.1.call-start = ((), (), s32[]{:S(2)}) async-start(), calls=%async_computation.3 | async-start | bytes 3543040
  689.6 67.5 %copy-start.3 = (f32[128,576]{0,1:T(8,128)S(1)}, f32[128,576]{0,1:T(8,128)}, u32[]{:S(2)}) copy-start(f32[128,576]{0,1:T(8,128)} %get-tuple-element.35) | copy-start | bytes 884740
  689.6 67.5 %copy-start.5 = (bf16[1536,576]{1,0:T(8,128)(2,1)S(1)}, bf16[1536,576]{1,0:T(8,128)(2,1)}, u32[]{:S(2)}) copy-start(bf16[1536,576]{1,0:T(8,128)(2,1)} %reshape.279) | copy-start | bytes 5308420
  689.6 67.5 %copy-start.18 = (bf16[128,1536]{1,0:T(8,128)(2,1)S(1)}, bf16[128,1536]{1,0:T(8,128)(2,1)}, u32[]{:S(2)}) copy-start(bf16[128,1536]{1,0:T(8,128)(2,1)} %get-tuple-element.19) | copy-start | bytes 1179652
  694.7 63.9 %copy-start.13 = (f32[128,576]{0,1:T(8,128)S(1)}, f32[128,576]{0,1:T(8,128)}, u32[]{:S(2)}) copy-start(f32[128,576]{0,1:T(8,128)} %copy-done.12) | copy-start | bytes 884740
  694.7 63.9 %copy-start.16 = (bf16[1,128,576]{1,2,0:T(8,128)(2,1)S(1)}, bf16[1,128,576]{1,2,0:T(8,128)(2,1)}, u32[]{:S(2)}) copy-start(bf16[1,128,576]{1,2,0:T(8,128)(2,1)} %param.6) | copy-start | bytes 442372
  694.7 63.9 %copy-start.31 = (f32[128,576]{0,1:T(8,128)S(1)}, f32[128,576]{0,1:T(8,128)}, u32[]{:S(2)}) copy-start(f32[128,576]{0,1:T(8,128)} %get-tuple-element.37) | copy-start | bytes 884740
  694.7 63.9 %copy-start.40 = (f32[576]{0:T(1024)S(1)}, f32[576]{0:T(1024)}, u32[]{:S(2)}) copy-start(f32[576]{0:T(1024)} %copy-done.38) | copy-start | bytes 6916
  694.7 63.9 %copy-start.50 = (f32[128]{0:T(128)S(1)}, f32[128]{0:T(128)}, u32[]{:S(2)}) copy-start(f32[128]{0:T(128)} %copy-done.49) | copy-start | bytes 1540
  694.7 95.9 %all-gather.3.cloned.1.call-start = ((), (), s32[]{:S(2)}) async-start(), calls=%async_computation.1 | async-start | bytes 3985920 | tf_op jit(solution)/shard_map/all_gather | solution.py:246
  (35 other events, 93.0 us)
Sparse Core Ops, SparseCore 0:
  41.8 251.4 all-reduce.6
  438.3 247.6 all-reduce.8
  694.8 58.8 all-reduce.10
  757.2 33.3 all-gather.2
where the time goes:
time: 868 us; the launch traced here: 859 us
  waiting for transfers between devices  587 us (68%)
  local copies, waits for them, and re-layouts  170 us (20%)
  other arithmetic  49.6 us (6%)
  matrix products  23.4 us (3%)
  between operations  16.6 us (2%)
  blocking collectives  12.3 us (1%)
    unnamed x7, waiting for transfers between devices  555 us
    concatenate x1, local copies, waits for them, and re-layouts, layer_row(): jnp.concatenate([grad_qkv.reshape(-1), grad_out.reshape(-1), grad_gateup....  87.1 us
    unnamed x115, local copies, waits for them, and re-layouts  43.6 us
    reduce_sum x1, other arithmetic, on_device(): squares = lax.psum(jnp.sum(summed * summed), 'group')  34.5 us
    all_gather x1, waiting for transfers between devices, on_device(): lax.all_gather(owned_piece.astype(jnp.bfloat16), 'wide', axis=0, tiled=True)  31.2 us
  transfers between devices with their start and end apart: 4, of which 4 were waited for; matrix products, arithmetic and copies ran while one was open for 0% of the time, Pallas kernels for 0%

commit v1 on v0

--- a/solution.py
+++ b/solution.py
@@ -1,9 +1,15 @@
+import functools
 import math
 
 import jax
 import jax.numpy as jnp
 from jax import lax
+from jax.experimental import pallas as pl
+from jax.experimental.pallas import tpu as pltpu
 from jax.sharding import PartitionSpec as P
+
+MESH = pl.DeviceIdType.MESH
+LANES = 128
 
 MODEL_WIDTH = 576
 QUERY_HEADS = 9
@@ -41,23 +47,21 @@
     )
 
 
-def unpack(flat):
+def unpack(main, gains):
     query_key_value_width = (QUERY_HEADS + 2 * KEY_VALUE_HEADS) * HEAD_SIZE
     shapes = [
         (MODEL_WIDTH, query_key_value_width),
         (QUERY_HEADS * HEAD_SIZE, MODEL_WIDTH),
         (MODEL_WIDTH, 2 * FF),
         (FF, MODEL_WIDTH),
-        (MODEL_WIDTH,),
-        (MODEL_WIDTH,),
     ]
     pieces = []
     offset = 0
     for piece_shape in shapes:
-        extent = math.prod(piece_shape)
-        pieces.append(flat[offset : offset + extent].reshape(piece_shape))
+        extent = math.prod(piece_shape) // LANES
+        pieces.append(main[offset : offset + extent].reshape(piece_shape))
         offset += extent
-    return pieces
+    return pieces + [gains[:MODEL_WIDTH], gains[MODEL_WIDTH:]]
 
 
 def positions_of(segment_row):
@@ -205,17 +209,10 @@
     d_inputs = (d_mid + norm_back(d_hidden_attn, normed_attn, inv_attn, gain_one)).astype(
         jnp.bfloat16
     )
-    flat_grads = jnp.concatenate(
-        [
-            grad_qkv.reshape(-1),
-            grad_out.reshape(-1),
-            grad_gateup.reshape(-1),
-            grad_down.reshape(-1),
-            grad_gain_attn,
-            grad_gain_ffn,
-        ]
-    )
-    return (outputs, d_inputs, flat_grads)
+    matrices = [grad_qkv, grad_out, grad_gateup, grad_down]
+    main = jnp.concatenate([m.astype(jnp.bfloat16).reshape(-1, LANES) for m in matrices])
+    gains = jnp.concatenate([grad_gain_attn, grad_gain_ffn])
+    return (outputs, d_inputs, main, gains)
 
 
 def adam_update(grads, clip_factor, params, moment_one, moment_two, decay_mask):
@@ -228,29 +225,383 @@
     return (new_params, new_moment_one, new_moment_two)
 
 
+def my_bits(wide, count):
+    return [(wide // 2**b) % 2 for b in range(count)]
+
+
+def flipped(wide, bit, b):
+    return wide + (1 - 2 * bit) * 2**b
+
+
+def greet(wide, group, bits, groups):
+    barrier = pltpu.get_barrier_semaphore()
+    peers = [(flipped(wide, bit, b), group) for b, bit in enumerate(bits)]
+    peers += [(wide, (group + d) % groups) for d in range(1, groups)]
+    for peer in peers:
+        pl.semaphore_signal(barrier, inc=1, device_id=peer, device_id_type=MESH)
+    pl.semaphore_wait(barrier, len(peers))
+
+
+def send(src, dst, send_sem, recv_sem, peer):
+    copy = pltpu.make_async_remote_copy(
+        src_ref=src,
+        dst_ref=dst,
+        send_sem=send_sem,
+        recv_sem=recv_sem,
+        device_id=peer,
+        device_id_type=MESH,
+    )
+    copy.start()
+    return copy
+
+
+def bit_order(chunk, count):
+    rest = list(range(1, count))
+    return [0] + (rest if chunk % 2 == 0 else rest[::-1])
+
+
+def tails_kernel(groups, bits_count, tail_ref, out_ref, send_sem, recv_sem):
+    wide, group = lax.axis_index("wide"), lax.axis_index("group")
+    greet(wide, group, [], groups)
+    out_ref[pl.ds(group, 1)] = tail_ref[...][None]
+    copies = []
+    for d in range(1, groups):
+        copies.append(
+            send(
+                tail_ref,
+                out_ref.at[group],
+                send_sem.at[d - 1],
+                recv_sem.at[d - 1],
+                (wide, (group + d) % groups),
+            )
+        )
+    for copy in copies:
+        copy.wait()
+
+
+def gather_kernel(groups, count, chunks, block_ref, out_ref, own_sem, zs, zr, ws, wr):
+    wide, group = lax.axis_index("wide"), lax.axis_index("group")
+    bits = my_bits(wide, count)
+    step = block_ref.shape[-2] // chunks
+    greet(wide, group, bits, groups)
+
+    def place(ref, lead, open_bits, chunk):
+        index = [slice(None) if b in open_bits else bits[b] for b in reversed(range(count))]
+        return ref.at[tuple(lead + index + [pl.ds(chunk * step, step)])]
+
+    units = [(d, c) for d in range(1, groups) for c in range(chunks)]
+    copies = {}
+    for u, (d, c) in enumerate(units):
+        copies[u, 0] = send(
+            place(block_ref, [], [], c),
+            place(out_ref, [group], [], c),
+            zs.at[u],
+            zr.at[u],
+            (wide, (group + d) % groups),
+        )
+    own = pltpu.make_async_copy(block_ref, out_ref.at[group], own_sem)
+    own.start()
+    for tick in range(len(units) // chunks + count + 1):
+        for u, (d, c) in enumerate(units):
+            stage = tick - u // chunks
+            if not 0 <= stage <= count:
+                continue
+            copies[u, stage].wait_recv()
+            if stage == count:
+                continue
+            order = bit_order(c, count)[::-1]
+            b = order[stage]
+            source = (group + groups - d) % groups
+            here = place(out_ref, [source], order[:stage], c)
+            copies[u, stage + 1] = send(
+                here, here, ws.at[u, stage], wr.at[u, stage], (flipped(wide, bits[b], b), group)
+            )
+    for copy in copies.values():
+        copy.wait_send()
+    own.wait()
+
+
+def sum_kernel(groups, count, chunks, x_ref, gain_ref, out_ref, head_ref, gsum_ref, sq_ref, *scratch):
+    recvs, accs = scratch[:count], scratch[count : 2 * count]
+    recv_z, gain_w, gain_z, sq_z, piece_head = scratch[2 * count : 2 * count + 5]
+    ss, sr, zs, zr, gs, gr, xs, xr, gzs, gzr, qs, qr, hs, hr = scratch[2 * count + 5 :]
+    wide, group = lax.axis_index("wide"), lax.axis_index("group")
+    bits = my_bits(wide, count)
+    step = x_ref.shape[-2] // chunks
+    greet(wide, group, bits, groups)
+    copies = {}
+    f32 = jnp.float32
+
+    def partner(b):
+        return (flipped(wide, bits[b], b), group)
+
+    def part(c, stage, value):
+        order = bit_order(c, count)
+        left = sorted(order[stage:], reverse=True)
+        return [value if b == order[stage] else slice(None) for b in left]
+
+    def held(c, stage):
+        return x_ref if stage == 0 else accs[stage - 1].at[c]
+
+    def view(c, stage, flip):
+        b = bit_order(c, count)[stage]
+        index = [slice(None)] + part(c, stage, 1 - bits[b] if flip else bits[b])
+        if stage == 0:
+            index += [slice(None)] * (count + 2 - len(index) - 1)
+            return x_ref.at[tuple(index + [pl.ds(c * step, step)])]
+        return accs[stage - 1].at[tuple([c] + index)]
+
+    def start_scatter(c, stage):
+        b = bit_order(c, count)[stage]
+        copies["s", c, stage] = send(
+            view(c, stage, True), recvs[stage].at[c], ss.at[c, stage], sr.at[c, stage], partner(b)
+        )
+
+    def add_scatter(c, stage):
+        copies["s", c, stage].wait_recv()
+        mine, other, total = view(c, stage, False), recvs[stage].at[c], accs[stage].at[c]
+
+        def body(i, _):
+            total[i] = (mine[i].astype(f32) + other[i].astype(f32)).astype(jnp.bfloat16)
+            return 0
+
+        lax.fori_loop(0, groups, body, 0)
+
+    def start_groups(c):
+        for d in range(1, groups):
+            to = (group + d) % groups
+            copies["z", c, d] = send(
+                accs[-1].at[c, to],
+                recv_z.at[c, d - 1],
+                zs.at[c, d - 1],
+                zr.at[c, d - 1],
+                (wide, to),
+            )
+
+    def place(open_bits, c):
+        index = [slice(None) if b in open_bits else bits[b] for b in reversed(range(count))]
+        return out_ref.at[tuple(index + [pl.ds(c * step, step)])]
+
+    def add_groups(c):
+        total = accs[-1][c, group].astype(f32)
+        for d in range(1, groups):
+            copies["z", c, d].wait_recv()
+            total = total + recv_z[c, d - 1].astype(f32)
+        place([], c)[...] = total.astype(jnp.bfloat16)
+
+    def start_gather(c, stage):
+        order = bit_order(c, count)[::-1]
+        here = place(order[:stage], c)
+        copies["g", c, stage] = send(
+            here, here, gs.at[c, stage], gr.at[c, stage], partner(order[stage])
+        )
+
+    for c in range(chunks):
+        start_scatter(c, 0)
+    gain_w[0] = gain_ref[...]
+    copies["x", 0] = send(gain_w.at[0], gain_w.at[count + 1], xs.at[0], xr.at[0], partner(0))
+
+    for tick in range(chunks // 2 + 2 * count + 1):
+        for c in range(chunks):
+            s = tick - c // 2
+            if 0 <= s < count:
+                add_scatter(c, s)
+                if s + 1 < count:
+                    start_scatter(c, s + 1)
+                else:
+                    start_groups(c)
+            elif s == count:
+                add_groups(c)
+                start_gather(c, 0)
+            elif count < s <= 2 * count:
+                copies["g", c, s - count - 1].wait_recv()
+                if s < 2 * count:
+                    start_gather(c, s - count)
+        if tick < count:
+            copies["x", tick].wait_recv()
+            gain_w[tick + 1] = gain_w[tick] + gain_w[count + 1 + tick]
+            if tick + 1 < count:
+                copies["x", tick + 1] = send(
+                    gain_w.at[tick + 1],
+                    gain_w.at[count + 2 + tick],
+                    xs.at[tick + 1],
+                    xr.at[tick + 1],
+                    partner(tick + 1),
+                )
+            else:
+                gain_z[pl.ds(group, 1)] = gain_w[pl.ds(count, 1)]
+                for d in range(1, groups):
+                    copies["gz", d] = send(
+                        gain_w.at[count],
+                        gain_z.at[group],
+                        gzs.at[d - 1],
+                        gzr.at[d - 1],
+                        (wide, (group + d) % groups),
+                    )
+
+    first = tuple([0] * count + [pl.ds(0, 16)])
+    copies["h"] = send(out_ref.at[first], head_ref, hs, hr, (wide, (group + groups - 1) % groups))
+    flat_lead = out_ref.shape[:-2]
+
+    def squares(i, total):
+        index = tuple((i // 2**b) % 2 for b in reversed(range(len(flat_lead))))
+        value = out_ref[index].astype(f32)
+        value = value * value
+        return total + jnp.sum(value.reshape(-1, 8, LANES), axis=0)
+
+    square = lax.fori_loop(0, math.prod(flat_lead), squares, jnp.zeros((8, LANES), f32))
+    piece_head[...] = square
+    sq_z[pl.ds(group, 1)] = square[None]
+    for d in range(1, groups):
+        copies["q", d] = send(
+            piece_head, sq_z.at[group], qs.at[d - 1], qr.at[d - 1], (wide, (group + d) % groups)
+        )
+    for d in range(1, groups):
+        copies["gz", d].wait_recv()
+    gains = gain_z[0]
+    for d in range(1, groups):
+        gains = gains + gain_z[d]
+    gsum_ref[...] = gains
+    for d in range(1, groups):
+        copies["q", d].wait_recv()
+    square = sq_z[0]
+    for d in range(1, groups):
+        square = square + sq_z[d]
+    sq_ref[...] = square
+    copies["h"].wait_recv()
+    for copy in copies.values():
+        copy.wait_send()
+
+
+def params_of(identity):
+    return pltpu.CompilerParams(
+        collective_id=identity, has_side_effects=True, vmem_limit_bytes=60 * 2**20
+    )
+
+
+def vmem_specs(n):
+    return [pl.BlockSpec(memory_space=pltpu.VMEM)] * n
+
+
+def gather_tails(tail, groups):
+    dma = pltpu.SemaphoreType.DMA
+    return pl.pallas_call(
+        functools.partial(tails_kernel, groups, 0),
+        out_shape=jax.ShapeDtypeStruct((groups,) + tail.shape, tail.dtype),
+        in_specs=vmem_specs(1),
+        out_specs=vmem_specs(1)[0],
+        scratch_shapes=[dma((groups - 1,)), dma((groups - 1,))],
+        compiler_params=params_of(0),
+        name="tails",
+    )(tail)
+
+
+def gather_blocks(block, groups, count, chunks):
+    dma = pltpu.SemaphoreType.DMA
+    units = (groups - 1) * chunks
+    return pl.pallas_call(
+        functools.partial(gather_kernel, groups, count, chunks),
+        out_shape=jax.ShapeDtypeStruct((groups,) + block.shape, block.dtype),
+        in_specs=vmem_specs(1),
+        out_specs=vmem_specs(1)[0],
+        scratch_shapes=[
+            dma,
+            dma((units,)),
+            dma((units,)),
+            dma((units, count)),
+            dma((units, count)),
+        ],
+        compiler_params=params_of(1),
+        name="gather_weights",
+    )(block)
+
+
+def sum_blocks(main, gains, groups, count, chunks):
+    dma = pltpu.SemaphoreType.DMA
+    rows = main.shape[-2]
+    step = rows // chunks
+    bf16, f32 = jnp.bfloat16, jnp.float32
+    stages = [
+        pltpu.VMEM((chunks, groups) + (2,) * (count - 1 - k) + (step, LANES), bf16)
+        for k in range(count)
+    ]
+    return pl.pallas_call(
+        functools.partial(sum_kernel, groups, count, chunks),
+        out_shape=(
+            jax.ShapeDtypeStruct((2,) * count + (rows, LANES), bf16),
+            jax.ShapeDtypeStruct((16, LANES), bf16),
+            jax.ShapeDtypeStruct(gains.shape, f32),
+            jax.ShapeDtypeStruct((8, LANES), f32),
+        ),
+        in_specs=vmem_specs(2),
+        out_specs=tuple(vmem_specs(4)),
+        scratch_shapes=stages
+        + stages
+        + [
+            pltpu.VMEM((chunks, groups - 1, step, LANES), bf16),
+            pltpu.VMEM((2 * count + 1,) + gains.shape, f32),
+            pltpu.VMEM((groups,) + gains.shape, f32),
+            pltpu.VMEM((groups, 8, LANES), f32),
+            pltpu.VMEM((8, LANES), f32),
+        ]
+        + [dma((chunks, count))] * 2
+        + [dma((chunks, groups - 1))] * 2
+        + [dma((chunks, count))] * 2
+        + [dma((count,))] * 2
+        + [dma((groups - 1,))] * 4
+        + [dma, dma],
+        compiler_params=params_of(2),
+        name="sum_grads",
+    )(main, gains)
+
+
 def on_device(inputs, segments, cotangent, params, moment_one, moment_two):
-    working = lax.all_gather(params.astype(jnp.bfloat16), "group", axis=0, tiled=True)
-    weights = unpack(working)
-    outputs, d_inputs, local_grads = layer_row(inputs[0], segments[0], cotangent[0], weights)
     groups = lax.axis_size("group")
     wides = lax.axis_size("wide")
+    group = lax.axis_index("group")
+    count = wides.bit_length() - 1
     share_len = params.shape[0]
-    piece_len = -(-share_len // wides)
-    shares = lax.psum_scatter(
-        local_grads.astype(jnp.bfloat16), "group", scatter_dimension=0, tiled=True
-    ).astype(jnp.float32)
-    padded = jnp.pad(shares, (0, piece_len * wides - share_len)).reshape(wides, piece_len)
-    owned_piece = lax.psum_scatter(
-        padded.astype(jnp.bfloat16), "wide", scatter_dimension=0, tiled=True
-    ).astype(jnp.float32)
-    collected_share = lax.all_gather(
-        owned_piece.astype(jnp.bfloat16), "wide", axis=0, tiled=True
-    ).astype(owned_piece.dtype)
-    summed = collected_share.reshape(-1)[:share_len]
-    squares = lax.psum(jnp.sum(summed * summed), "group")
+    gain_len = 2 * MODEL_WIDTH
+    extra = gain_len // groups
+    block_len = share_len - extra
+    block_rows = block_len // LANES
+    piece_rows = -(-block_rows // wides)
+    chunks = 6 if piece_rows % 96 == 0 else 2
+    piece_rows = -(-piece_rows // (16 * chunks)) * 16 * chunks
+    padding = piece_rows * wides - block_rows
+    lead = (2,) * count
+
+    def to_pieces(rows):
+        rows = rows.reshape(-1, block_rows, LANES)
+        if padding:
+            rows = jnp.pad(rows, ((0, 0), (0, padding), (0, 0)))
+        return rows.reshape((-1,) + lead + (piece_rows, LANES))
+
+    def from_pieces(pieces):
+        rows = pieces.reshape(-1, piece_rows * wides, LANES)[:, :block_rows]
+        return rows.reshape(-1, LANES)
+
+    rounded = params.astype(jnp.bfloat16)
+    tail = jnp.pad(rounded[share_len - gain_len :], (0, 16 * LANES - gain_len)).reshape(16, LANES)
+    tails = gather_tails(tail, groups).reshape(groups, -1)[:, :gain_len]
+    before = lax.dynamic_index_in_dim(tails, (group + groups - 1) % groups, keepdims=False)
+    joined = jnp.concatenate([before, rounded])
+    block = lax.dynamic_slice(joined, (gain_len - extra * group,), (block_len,))
+    gathered = gather_blocks(to_pieces(block)[0], groups, count, 2)
+    weights = unpack(from_pieces(gathered), tails[groups - 1])
+    outputs, d_inputs, main, gains = layer_row(inputs[0], segments[0], cotangent[0], weights)
+    gains = gains.astype(jnp.bfloat16).astype(jnp.float32)
+    gains = jnp.pad(gains, (0, 16 * LANES - gain_len)).reshape(16, LANES)
+    summed_block, head, gains, square = sum_blocks(to_pieces(main), gains, groups, count, chunks)
+    gains = gains.reshape(-1)[:gain_len].astype(jnp.bfloat16)
+    head = jnp.where(group == groups - 1, gains, head.reshape(-1)[:gain_len])
+    joined = jnp.concatenate([from_pieces(summed_block).reshape(-1), head])
+    summed = lax.dynamic_slice(joined, (extra * group,), (share_len,)).astype(jnp.float32)
+    gains = gains.astype(jnp.float32)
+    squares = jnp.sum(square) + jnp.sum(gains * gains)
     clip_factor = jnp.minimum(jnp.float32(1.0), max_norm * lax.rsqrt(squares))
-    flat_index = lax.axis_index("group") * share_len + jnp.arange(share_len, dtype=jnp.int32)
-    decay_mask = flat_index < share_len * groups - 2 * MODEL_WIDTH
+    flat_index = group * share_len + jnp.arange(share_len, dtype=jnp.int32)
+    decay_mask = flat_index < share_len * groups - gain_len
     new_params, new_moment_one, new_moment_two = adam_update(
         summed, clip_factor, params, moment_one, moment_two, decay_mask
     )

time: 868 us -> 221 us (0.25); the launches traced: 859 us -> 220 us
  waiting for transfers between devices: 587 us -> 0 us
  local copies, waits for them, and re-layouts: 170 us -> 38.3 us
  Pallas kernels: 0 us -> 121 us
  between operations: 16.6 us -> 3.37 us
  blocking collectives: 12.3 us -> 0 us
  other arithmetic: 49.6 us -> 37.8 us
    unnamed x7 -> x0, waiting for transfers between devices: 555 us -> none
    pallas_call x0 -> x3, Pallas kernels: none -> 121 us  [the longest x1 67.9 us: sum_blocks(): pl.pallas_call(functools.partial(sum_kernel, groups, count, chunks), out_...]
    concatenate x1 -> x0, local copies, waits for them, and re-layouts: 87.1 us -> none  [layer_row(): jnp.concatenate([grad_qkv.reshape(-1), grad_out.reshape(-1), grad_gateup....]
    unnamed x115 -> x89, local copies, waits for them, and re-layouts: 43.6 us -> 1.07 us
    reduce_sum x1 -> x2, other arithmetic: 34.5 us -> 2.59 us  [on_device(): squares = jnp.sum(square) + jnp.sum(gains * gains)]
    all_gather x1 -> x0, waiting for transfers between devices: 31.2 us -> none  [on_device(): lax.all_gather(owned_piece.astype(jnp.bfloat16), 'wide', axis=0, tiled=True)]
    concatenate x0 -> x2, other arithmetic: none -> 15 us  [the longest x1 12.3 us: layer_row(): jnp.concatenate([m.astype(jnp.bfloat16).reshape(-1, LANES) for m in matri...]
    psum x1 -> x0, blocking collectives: 12.3 us -> none  [on_device(): squares = lax.psum(jnp.sum(summed * summed), 'group')]
  transfers between devices with their start and end apart: 4 -> 0, of which waited for: 4 -> 0; matrix products, arithmetic and copies ran while one was open for 0% -> 0% of each run, Pallas kernels for 0% -> 0%
where the time goes in v1:
time: 221 us; the launch traced here: 220 us
  Pallas kernels  121 us (55%)
  local copies, waits for them, and re-layouts  38.3 us (17%)
  other arithmetic  37.8 us (17%)
  matrix products  19.8 us (9%)
  between operations  3.37 us (2%)
    pallas_call x1, Pallas kernels, sum_blocks(): pl.pallas_call(functools.partial(sum_kernel, groups, count, chunks), out_...  67.9 us
    pallas_call x1, Pallas kernels, gather_blocks(): pl.pallas_call(functools.partial(gather_kernel, groups, count, chunks), o...  44.7 us
    reshape x4, local copies, waits for them, and re-layouts, unpack(): pieces.append(main[offset:offset + extent].reshape(piece_shape))  13.9 us
    concatenate x1, other arithmetic, layer_row(): jnp.concatenate([m.astype(jnp.bfloat16).reshape(-1, LANES) for m in matri...  12.3 us
    sub x1, other arithmetic, adam_update(): new_params = params - learn_rate * (step_size + decay_term)  11.3 us
    reshape x4, local copies, waits for them, and re-layouts, layer_row(): m.astype(jnp.bfloat16).reshape(-1, LANES)  10.6 us
    pallas_call x1, Pallas kernels, gather_tails(): pl.pallas_call(functools.partial(tails_kernel, groups, 0), out_shape=jax....  8.6 us
    slice x4, local copies, waits for them, and re-layouts, unpack(): pieces.append(main[offset:offset + extent].reshape(piece_shape))  8.47 us

profile of v1, /device:TPU:0, one launch (start us, length us, event | category | flops | bytes accessed | tf_op | source)
XLA Modules:
  0.0 220.5 jit_solution(15412334418717841157)
XLA Ops:
  5.1 2.2 convert_element_type.106
  8.0 8.6 %tails.1 = bf16[4,16,128]{2,1,0:T(8,128)(2,1)} custom-call(bf16[16,128]{1,0:T(8,128)(2,1)} %pad_bitcast_fusion.tail_ref), custom_call_target="tpu_custom_call" | custom-call | tf_op jit(solution)/shard_map/tails/pallas_call | solution.py:488
  18.0 2.6 %fusion.4 = bf16[884736]{0:T(1024)(128)(2,1)} fusion(s32[]{:T(128)S(6)} %select_n.50, bf16[1152]{0:T(1024)(128)(2,1)S(1)} %dynamic-slice_reduce_fusion, bf16[885024]{0:T(1024)(128)(2,1)S(1)} %convert_element_type.106), kind=kLoop, calls=%fused_computation.16 | loop fusion | flops 3538944 | bytes 3541828 | tf_op jit(solution)/shard_map/concatenate | solution.py:588
  20.7 44.7 %gather_weights.1 = bf16[4,2,2,2,864,128]{5,4,3,2,1,0:T(8,128)(2,1)} custom-call(bf16[2,2,2,864,128]{4,3,2,1,0:T(8,128)(2,1)} %bitcast.146), custom_call_target="tpu_custom_call" | custom-call | tf_op jit(solution)/shard_map/gather_weights/pallas_call | solution.py:502
  68.0 2.5 %slice.116 = bf16[4320,128]{1,0:T(8,128)(2,1)} slice(bf16[27648,128]{1,0:T(8,128)(2,1)} %bitcast.142), slice={[0:4320], [0:128]} | slice | bytes 2211840 | tf_op jit(solution)/shard_map/slice | solution.py:62
  70.5 3.2 %reshape.272 = bf16[576,960]{1,0:T(8,128)(2,1)} reshape(bf16[4320,128]{1,0:T(8,128)(2,1)} %slice.116) | data formatting | bytes 2211840 | tf_op jit(solution)/shard_map/reshape | solution.py:62
  73.7 2.1 fusion.44
  78.6 2.8 %slice.106 = bf16[1,2,2,2,864,128]{5,4,3,2,1,0:T(8,128)(2,1)} slice(bf16[4,2,2,2,864,128]{5,4,3,2,1,0:T(8,128)(2,1)} %gather_weights.1), slice={[3:4], [0:2], [0:2], [0:2], [0:864], [0:128]} | slice | bytes 3538944 | tf_op jit(solution)/shard_map/slice | solution.py:62
  81.4 2.0 slice.103
  83.5 5.0 %reshape.278 = bf16[576,3072]{1,0:T(8,128)(2,1)S(1)} reshape(bf16[2,2,2,2,864,128]{5,4,3,2,1,0:T(8,128)(2,1)} %slice.103) | data formatting | bytes 7077888 | tf_op jit(solution)/shard_map/reshape | solution.py:62
  88.5 4.3 %reshape.279 = bf16[1536,576]{1,0:T(8,128)(2,1)} reshape(bf16[1,2,2,2,864,128]{5,4,3,2,1,0:T(8,128)(2,1)} %slice.106) | data formatting | bytes 3538944 | tf_op jit(solution)/shard_map/reshape | solution.py:62
  92.8 2.0 fusion.78
  97.4 1.8 multiply_reduce_fusion.1
  100.5 1.6 convolution_bitcast_fusion.3
  106.3 1.6 reshape.286
  108.5 2.4 %reshape.285 = bf16[4320,128]{1,0:T(8,128)(2,1)} reshape(bf16[576,960]{1,0:T(8,128)(2,1)S(1)} %convolution_convert_fusion.2) | data formatting | bytes 2211840 | tf_op jit(solution)/shard_map/reshape | solution.py:213
  110.9 1.8 convolution_convert_fusion.1
  112.7 2.7 %copy.26 = bf16[1536,576]{1,0:T(8,128)(2,1)S(1)} copy(bf16[1536,576]{0,1:T(8,128)(2,1)} %convolution_convert_fusion.1) | data formatting | bytes 3538944 | tf_op jit(solution)/shard_map/convert_element_type | solution.py:213
  115.4 3.0 %reshape.288 = bf16[6912,128]{1,0:T(8,128)(2,1)} reshape(bf16[1536,576]{1,0:T(8,128)(2,1)S(1)} %copy.26) | data formatting | bytes 3538944 | tf_op jit(solution)/shard_map/reshape | solution.py:213
  118.5 2.3 %convolution_convert_fusion = bf16[576,3072]{1,0:T(8,128)(2,1)S(1)} fusion(bf16[128,1536]{1,0:T(8,128)(2,1)} %copy-done.21, bf16[128,1536]{1,0:T(8,128)(2,1)} %copy-done.20, f32[128,576]{0,1:T(8,128)} %get-tuple-element.40, f32[576]{0:T(1024)S(1)} %copy-done.23, f32[128]{0:T(128)S(1)} %copy-done.38), kind=kOutput, calls=%fused_computation.3 | convolution fusion | flops 456548352 | bytes 4623104 | tf_op jit(solution)/shard_map/dot_general | solution.py:39
  120.8 3.6 %reshape.287 = bf16[13824,128]{1,0:T(8,128)(2,1)} reshape(bf16[576,3072]{1,0:T(8,128)(2,1)S(1)} %convolution_convert_fusion) | data formatting | bytes 7077888 | tf_op jit(solution)/shard_map/reshape | solution.py:213
  124.4 12.3 %pad_maximum_fusion = bf16[27648,128]{1,0:T(8,128)(2,1)} fusion(bf16[6912,128]{1,0:T(8,128)(2,1)} %reshape.288, bf16[13824,128]{1,0:T(8,128)(2,1)} %reshape.287, bf16[2592,128]{1,0:T(8,128)(2,1)} %reshape.286, bf16[4320,128]{1,0:T(8,128)(2,1)} %reshape.285), kind=kLoop, calls=%fused_computation.1 | loop fusion | flops 28311552 | bytes 14155776 | tf_op jit(solution)/shard_map/concatenate | solution.py:213
  136.7 67.9 %sum_grads.1 = (bf16[2,2,2,864,128]{4,3,2,1,0:T(8,128)(2,1)}, bf16[16,128]{1,0:T(8,128)(2,1)}, f32[16,128]{1,0:T(8,128)}, f32[8,128]{1,0:T(8,128)}) custom-call(bf16[4,2,2,2,864,128]{5,4,3,2,1,0:T(8,128)(2,1)} %bitcast.145, f32[16,128]{1,0:T(8,128)} %fusion.64.gain_ref), custom_call_target="tpu_custom_call" | custom-call | tf_op jit(solution)/shard_map/sum_grads/pallas_call | solution.py:528
  209.2 11.3 %multiply_subtract_fusion = (f32[885024]{0:T(1024)}, f32[885024]{0:T(1024)}, f32[885024]{0:T(1024)}, f32[885024]{0:T(1024)}) fusion(f32[885024]{0:T(1024)S(1)} %copy-done, s32[]{:T(128)S(6)} %mul.404, f32[]{:T(128)S(6)} %min.3, f32[885024]{0:T(1024)} %param.10, f32[885024]{0:T(1024)} %param.11, s32[]{:T(128)S(6)} %select_n.56, ...), kind=kLoop, calls=%fused_computation.5 | loop fusion | flops 20355552 | bytes 26552460 | tf_op jit(solution)/shard_map/sub | solution.py:224
  (140 shorter events, 22.8 us)
Async XLA Ops:
  3.7 70.0 %copy-start.39 = (f32[128]{0:T(128)}, f32[128]{0:T(128)S(1)}, u32[]{:S(2)}) copy-start(f32[128]{0:T(128)S(1)} %add_rsqrt_fusion.1) | copy-start | bytes 1540
  5.1 70.8 %copy-start.18 = (f32[128,32]{0,1:T(8,128)}, f32[128,32]{0,1:T(8,128)S(1)}, u32[]{:S(2)}) copy-start(f32[128,32]{0,1:T(8,128)S(1)} %get-tuple-element.36) | copy-start | bytes 49156
  18.0 55.7 %copy-start.28 = (f32[576]{0:T(1024)}, f32[576]{0:T(1024)S(1)}, u32[]{:S(2)}) copy-start(f32[576]{0:T(1024)S(1)} %get-tuple-element.19) | copy-start | bytes 6916
  65.4 8.3 %copy-start.8 = (bf16[1,128,576]{1,2,0:T(8,128)(2,1)S(1)}, bf16[1,128,576]{1,2,0:T(8,128)(2,1)}, u32[]{:S(2)}) copy-start(bf16[1,128,576]{1,2,0:T(8,128)(2,1)} %param.6) | copy-start | bytes 442372
  68.0 13.4 %slice-start = ((s8[7077888]{0:T(1024)(128)(4,1)}), s8[2883584]{0:T(1024)(128)(4,1)S(1)}, s32[]{:S(2)}) async-start(s8[7077888]{0:T(1024)(128)(4,1)} %bitcast.143), calls=%async_computation | async-start | bytes 5767168
  75.8 5.6 %slice-start.1 = ((s8[7077888]{0:T(1024)(128)(4,1)}), s8[4194304]{0:T(1024)(128)(4,1)S(1)}, s32[]{:S(2)}) async-start(s8[7077888]{0:T(1024)(128)(4,1)} %bitcast.143), calls=%async_computation.1 | async-start | bytes 8388608
  76.0 5.4 %copy-start.33 = (bf16[128,3,32]{0,2,1:T(8,128)(2,1)}, bf16[128,3,32]{0,2,1:T(8,128)(2,1)S(1)}, u32[]{:S(2)}) copy-start(bf16[128,3,32]{0,2,1:T(8,128)(2,1)S(1)} %get-tuple-element.33) | copy-start | bytes 73732
  76.0 5.4 %copy-start.35 = (bf16[128,3,32]{0,2,1:T(8,128)(2,1)}, bf16[128,3,32]{0,2,1:T(8,128)(2,1)S(1)}, u32[]{:S(2)}) copy-start(bf16[128,3,32]{0,2,1:T(8,128)(2,1)S(1)} %get-tuple-element.34) | copy-start | bytes 73732
  76.6 4.8 %copy-start.30 = (f32[3,3,128]{2,1,0:T(4,128)}, f32[3,3,128]{2,1,0:T(4,128)S(1)}, u32[]{:S(2)}) copy-start(f32[3,3,128]{2,1,0:T(4,128)S(1)} %log_add_fusion) | copy-start | bytes 13828
  95.9 3.3 %copy-start.10 = (bf16[128,1536]{1,0:T(8,128)(2,1)}, bf16[128,1536]{1,0:T(8,128)(2,1)S(1)}, u32[]{:S(2)}) copy-start(bf16[128,1536]{1,0:T(8,128)(2,1)S(1)} %get-tuple-element.26) | copy-start | bytes 1179652
  95.9 3.3 %copy-start.20 = (bf16[128,1536]{1,0:T(8,128)(2,1)}, bf16[128,1536]{1,0:T(8,128)(2,1)S(1)}, u32[]{:S(2)}) copy-start(bf16[128,1536]{1,0:T(8,128)(2,1)S(1)} %get-tuple-element.24) | copy-start | bytes 1179652
  95.9 3.3 %copy-start.21 = (bf16[128,1536]{1,0:T(8,128)(2,1)}, bf16[128,1536]{1,0:T(8,128)(2,1)S(1)}, u32[]{:S(2)}) copy-start(bf16[128,1536]{1,0:T(8,128)(2,1)S(1)} %get-tuple-element.25) | copy-start | bytes 1179652
  99.2 4.5 %copy-start.19 = (f32[128,32]{0,1:T(8,128)S(1)}, f32[128,32]{0,1:T(8,128)}, u32[]{:S(2)}) copy-start(f32[128,32]{0,1:T(8,128)} %copy-done.18) | copy-start | bytes 49156
  99.3 4.6 %copy-start.7 = (bf16[576,960]{1,0:T(8,128)(2,1)S(1)}, bf16[576,960]{1,0:T(8,128)(2,1)}, u32[]{:S(2)}) copy-start(bf16[576,960]{1,0:T(8,128)(2,1)} %reshape.272) | copy-start | bytes 3317764
  99.3 4.6 %copy-start.9 = (bf16[1,128,576]{1,2,0:T(8,128)(2,1)S(1)}, bf16[1,128,576]{1,2,0:T(8,128)(2,1)}, u32[]{:S(2)}) copy-start(bf16[1,128,576]{1,2,0:T(8,128)(2,1)} %param.6) | copy-start | bytes 442372
  99.3 4.6 %copy-start.29 = (f32[576]{0:T(1024)S(1)}, f32[576]{0:T(1024)}, u32[]{:S(2)}) copy-start(f32[576]{0:T(1024)} %copy-done.28) | copy-start | bytes 6916
  99.3 4.6 %copy-start.40 = (f32[128]{0:T(128)S(1)}, f32[128]{0:T(128)}, u32[]{:S(2)}) copy-start(f32[128]{0:T(128)} %copy-done.39) | copy-start | bytes 1540
  100.1 5.2 %copy-start.41 = (bf16[576]{0:T(1024)(128)(2,1)S(1)}, bf16[576]{0:T(1024)(128)(2,1)}, u32[]{:S(2)}) copy-start(bf16[576]{0:T(1024)(128)(2,1)} %get-tuple-element.14) | copy-start | bytes 3460
  100.1 5.8 %copy-start.13 = (bf16[3,64,3,128]{3,1,2,0:T(8,128)(2,1)S(1)}, bf16[3,64,3,128]{3,1,2,0:T(8,128)(2,1)}, u32[]{:S(2)}) copy-start(bf16[3,64,3,128]{3,1,2,0:T(8,128)(2,1)} %copy-done.12) | copy-start | bytes 442372
  104.5 6.4 %copy-start.11 = (bf16[128,1536]{1,0:T(8,128)(2,1)S(1)}, bf16[128,1536]{1,0:T(8,128)(2,1)}, u32[]{:S(2)}) copy-start(bf16[128,1536]{1,0:T(8,128)(2,1)} %copy-done.10) | copy-start | bytes 1179652
  104.5 6.4 %copy-start.15 = (bf16[1,128,576]{1,2,0:T(8,128)(2,1)S(1)}, bf16[1,128,576]{1,2,0:T(8,128)(2,1)}, u32[]{:S(2)}) copy-start(bf16[1,128,576]{1,2,0:T(8,128)(2,1)} %param.8) | copy-start | bytes 442372
  112.7 5.8 %copy-start.23 = (f32[576]{0:T(1024)S(1)}, f32[576]{0:T(1024)}, u32[]{:S(2)}) copy-start(f32[576]{0:T(1024)} %get-tuple-element.18) | copy-start | bytes 6916
  112.7 5.8 %copy-start.38 = (f32[128]{0:T(128)S(1)}, f32[128]{0:T(128)}, u32[]{:S(2)}) copy-start(f32[128]{0:T(128)} %add_rsqrt_fusion) | copy-start | bytes 1540
  136.7 72.5 %copy-start = (f32[885024]{0:T(1024)S(1)}, f32[885024]{0:T(1024)}, u32[]{:S(2)}) copy-start(f32[885024]{0:T(1024)} %param.9) | copy-start | bytes 10620292
  (20 other events, 39.2 us)

commit v2 on v1

--- a/solution.py
+++ b/solution.py
@@ -483,7 +483,7 @@
     return [pl.BlockSpec(memory_space=pltpu.VMEM)] * n
 
 
-def gather_tails(tail, groups):
+def gather_tails(tail, groups, identity):
     dma = pltpu.SemaphoreType.DMA
     return pl.pallas_call(
         functools.partial(tails_kernel, groups, 0),
@@ -491,7 +491,7 @@
         in_specs=vmem_specs(1),
         out_specs=vmem_specs(1)[0],
         scratch_shapes=[dma((groups - 1,)), dma((groups - 1,))],
-        compiler_params=params_of(0),
+        compiler_params=params_of(identity),
         name="tails",
     )(tail)
 
@@ -555,6 +555,280 @@
     )(main, gains)
 
 
+def dot(left_op, right_op, left_dim, right_dim):
+    return lax.dot_general(
+        left_op,
+        right_op,
+        (((left_dim,), (right_dim,)), ((), ())),
+        preferred_element_type=jnp.float32,
+    )
+
+
+def layer_kernel(
+    x_ref, seg_ref, cot_ref, w_ref, gain_ref, freq_ref,
+    out_ref, din_ref, main_ref, gg_ref,
+    att_s, mid_s, hid_s, down_s, dhid_s, dproj_s, dmid_s,
+):
+    f32, bf16 = jnp.float32, jnp.bfloat16
+    width, length, half = MODEL_WIDTH, x_ref.shape[0], HEAD_SIZE // 2
+    part = width // 2
+    heads, kv = QUERY_HEADS, KEY_VALUE_HEADS
+    repeat = heads // kv
+    scale = HEAD_SIZE**-0.5
+    first_panel = (heads * HEAD_SIZE) // LANES
+
+    def zero_panel(p):
+        return w_ref[0, pl.ds(p * width, width), :]
+
+    def zero_pair(p):
+        return jnp.concatenate([zero_panel(p), zero_panel(p + 1)], axis=-1)
+
+    gain_one, gain_two = gain_ref[0:1, :], gain_ref[1:2, :]
+    x = x_ref[...].astype(f32)
+    inv_attn = lax.rsqrt(jnp.mean(x * x, axis=-1, keepdims=True) + norm_eps)
+    normed_attn = x * inv_attn
+    hidden_attn = (normed_attn * gain_one).astype(bf16)
+
+    seg_row = jnp.broadcast_to(seg_ref[...].astype(f32), (length, length))
+    rows = lax.broadcasted_iota(jnp.int32, (length, length), 0)
+    columns = lax.broadcasted_iota(jnp.int32, (length, length), 1)
+    allowed = (seg_row == seg_row.T) & (rows >= columns)
+    positions = jnp.sum(jnp.where(allowed, 1.0, 0.0), axis=-1, keepdims=True) - 1.0
+    angles = positions * freq_ref[...]
+    lane = lax.broadcasted_iota(jnp.int32, (length, LANES), 1)
+    first = lane % HEAD_SIZE < half
+    cosine, sine = jnp.cos(angles), jnp.sin(angles)
+    sine = jnp.where(first, -sine, sine)
+
+    def swap(u):
+        return jnp.where(first, pltpu.roll(u, LANES - half, 1), pltpu.roll(u, half, 1))
+
+    plain = {}
+    panels = 12
+    for p in range(first_panel, panels, 2):
+        both = dot(hidden_attn, zero_pair(p), 1, 0)
+        plain[p], plain[p + 1] = both[:, :LANES], both[:, LANES:]
+    turned = {p: u * cosine + swap(u) * sine for p, u in plain.items()}
+
+    def slot(source, s):
+        at = s % 2 * HEAD_SIZE
+        return source[s // 2][:, at : at + HEAD_SIZE].astype(bf16)
+
+    mask = jnp.concatenate([allowed] * repeat, axis=0)
+    saved = []
+    for j in range(kv):
+        queries = jnp.concatenate([slot(turned, heads + repeat * j + r) for r in range(repeat)], axis=0)
+        keys, values = slot(turned, 2 * heads + j), slot(plain, 2 * heads + kv + j)
+        scores = jnp.where(mask, dot(queries, keys, 1, 1) * scale, masked_value)
+        peak = jnp.max(scores, axis=-1, keepdims=True)
+        total = jnp.sum(jnp.exp(scores - peak), axis=-1, keepdims=True)
+        probs = jnp.exp(scores - (peak + jnp.log(total)))
+        probs_b = probs.astype(bf16)
+        attended = dot(probs_b, values, 1, 0)
+        for r in range(repeat):
+            at = (repeat * j + r) * HEAD_SIZE
+            att_s[:, at : at + HEAD_SIZE] = attended[r * length : (r + 1) * length].astype(bf16)
+        saved.append((queries, keys, values, probs, probs_b))
+
+    attended = att_s[...]
+    for p in range(0, first_panel, 2):
+        at = p * LANES
+        mid_s[:, at : at + 2 * LANES] = dot(attended, zero_pair(p), 1, 0)
+    at = first_panel * LANES
+    mid_s[:, at:width] = dot(attended, zero_panel(first_panel), 1, 0)[:, : width - at]
+    mid = x + mid_s[...]
+    inv_ffn = lax.rsqrt(jnp.mean(mid * mid, axis=-1, keepdims=True) + norm_eps)
+    normed_ffn = mid * inv_ffn
+    hid_s[...] = (normed_ffn * gain_two).astype(bf16)
+    mid_s[...] = mid
+    down_s[...] = jnp.zeros_like(down_s)
+    dhid_s[...] = jnp.zeros_like(dhid_s)
+
+    def gateup_rows(p):
+        return pl.ds(pl.multiple_of(p * part, part), part)
+
+    def gateup_pair(p):
+        sides = [
+            jnp.concatenate([w_ref[1, gateup_rows(q), :], w_ref[2, gateup_rows(q), :]], axis=0)
+            for q in (p, p + 1)
+        ]
+        return jnp.concatenate(sides, axis=-1)
+
+    def store_gateup(p, value):
+        value = value.astype(bf16)
+        for q in range(2):
+            columns = slice(q * LANES, (q + 1) * LANES)
+            main_ref[1, gateup_rows(p + q), :] = value[:part, columns]
+            main_ref[2, gateup_rows(p + q), :] = value[part:, columns]
+
+    half_panels = FF // LANES
+
+    def hidden_step(i, _):
+        p = 2 * i
+        hidden, cotangent = hid_s[...], cot_ref[...]
+        gate_w, up_w = gateup_pair(p), gateup_pair(p + half_panels)
+        down_rows = [pl.ds(pl.multiple_of((p + q) * width, width), width) for q in range(2)]
+        down_w = jnp.concatenate([w_ref[3, r, :] for r in down_rows], axis=-1)
+        gate, upper = dot(hidden, gate_w, 1, 0), dot(hidden, up_w, 1, 0)
+        d_act = dot(cotangent, down_w, 1, 0)
+        sigmoid = jax.nn.sigmoid(gate)
+        activation = (gate * sigmoid * upper).astype(bf16)
+        d_gate = (d_act * upper * sigmoid * (1.0 + gate * (1.0 - sigmoid))).astype(bf16)
+        d_upper = (d_act * gate * sigmoid).astype(bf16)
+        down_s[...] += dot(activation, down_w, 1, 1)
+        dhid_s[...] += dot(d_gate, gate_w, 1, 1) + dot(d_upper, up_w, 1, 1)
+        store_gateup(p, dot(hidden, d_gate, 0, 0))
+        store_gateup(p + half_panels, dot(hidden, d_upper, 0, 0))
+        d_down = dot(cotangent, activation, 0, 0).astype(bf16)
+        for q in range(2):
+            main_ref[3, down_rows[q], :] = d_down[:, q * LANES : (q + 1) * LANES]
+        return 0
+
+    lax.fori_loop(0, half_panels // 2, hidden_step, 0)
+    mid = mid_s[...]
+    normed_ffn = mid * inv_ffn
+    out_ref[...] = (mid + down_s[...]).astype(bf16)
+    d_hidden = dhid_s[...]
+    gg_ref[1:2, :] = jnp.sum(d_hidden * normed_ffn, axis=0, keepdims=True)
+    d_mid = cot_ref[...].astype(f32) + norm_back(d_hidden, normed_ffn, inv_ffn, gain_two)
+    dmid_s[...] = jnp.zeros_like(dmid_s)
+    dmid_s[:, :width] = d_mid.astype(bf16)
+    attended = att_s[...]
+    d_attended = jnp.zeros((length, width), f32)
+    for p in range(0, first_panel + 2, 2):
+        at = p * LANES
+        if p == first_panel:
+            block = dmid_s[:, at : at + LANES]
+            d_attended += dot(block, zero_panel(p), 1, 1)
+        else:
+            block = dmid_s[:, at : at + 2 * LANES]
+            d_attended += dot(block, zero_pair(p), 1, 1)
+        value = dot(attended, block, 0, 0)
+        if p == first_panel:
+            edge = value
+        else:
+            main_ref[0, pl.ds(p * width, width), :] = value[:, :LANES].astype(bf16)
+            main_ref[0, pl.ds((p + 1) * width, width), :] = value[:, LANES:].astype(bf16)
+    att_s[...] = d_attended.astype(bf16)
+
+    dproj_s[...] = jnp.zeros_like(dproj_s)
+    start = first_panel * 2
+    for j in range(kv):
+        queries, keys, values, probs, probs_b = saved[j]
+        d_att = jnp.concatenate(
+            [
+                att_s[:, (repeat * j + r) * HEAD_SIZE : (repeat * j + r + 1) * HEAD_SIZE]
+                for r in range(repeat)
+            ],
+            axis=0,
+        )
+        d_probs = dot(d_att, values, 1, 1)
+        row_total = jnp.sum(probs * d_probs, axis=-1, keepdims=True)
+        d_scores = (probs * (d_probs - row_total) * scale).astype(bf16)
+        d_queries = dot(d_scores, keys, 1, 0)
+        for r in range(repeat):
+            at = (heads + repeat * j + r - start) * HEAD_SIZE
+            dproj_s[:, at : at + HEAD_SIZE] = d_queries[r * length : (r + 1) * length]
+        at = (2 * heads + j - start) * HEAD_SIZE
+        dproj_s[:, at : at + HEAD_SIZE] = dot(d_scores, queries, 0, 0)
+        at = (2 * heads + kv + j - start) * HEAD_SIZE
+        dproj_s[:, at : at + HEAD_SIZE] = dot(probs_b, d_att, 0, 0)
+
+    turned_lanes = (2 * heads + kv - start) * HEAD_SIZE
+    d_hidden = jnp.zeros((length, width), f32)
+    for p in range(first_panel, panels, 2):
+        sides = []
+        for q in (p, p + 1):
+            at = (q - first_panel) * LANES
+            raw = dproj_s[:, at : at + LANES]
+            back = raw * cosine - swap(raw) * sine
+            sides.append(jnp.where(lane + at < turned_lanes, back, raw).astype(bf16))
+        both = jnp.concatenate(sides, axis=-1)
+        d_hidden += dot(both, zero_pair(p), 1, 1)
+        value = dot(hidden_attn, both, 0, 0)
+        left = value[:, :LANES]
+        if p == first_panel:
+            left = left + edge
+        main_ref[0, pl.ds(p * width, width), :] = left.astype(bf16)
+        main_ref[0, pl.ds((p + 1) * width, width), :] = value[:, LANES:].astype(bf16)
+    gg_ref[0:1, :] = jnp.sum(d_hidden * normed_attn, axis=0, keepdims=True)
+    din_ref[...] = (d_mid + norm_back(d_hidden, normed_attn, inv_attn, gain_one)).astype(bf16)
+
+
+def layer_panels(inputs, segment_row, cotangent, weights, gains):
+    length = inputs.shape[0]
+    half = HEAD_SIZE // 2
+    f32, bf16 = jnp.float32, jnp.bfloat16
+    freqs = theta_base ** (-2.0 * jnp.arange(half, dtype=f32) / HEAD_SIZE)
+    freqs = jnp.tile(freqs, LANES // half)[None]
+    full = (length, MODEL_WIDTH)
+    kept = (QUERY_HEADS * HEAD_SIZE) // LANES * LANES
+    return pl.pallas_call(
+        layer_kernel,
+        out_shape=(
+            jax.ShapeDtypeStruct(full, bf16),
+            jax.ShapeDtypeStruct(full, bf16),
+            jax.ShapeDtypeStruct(weights.shape, bf16),
+            jax.ShapeDtypeStruct((2, MODEL_WIDTH), f32),
+        ),
+        in_specs=vmem_specs(6),
+        out_specs=tuple(vmem_specs(4)),
+        scratch_shapes=[
+            pltpu.VMEM(full, bf16),
+            pltpu.VMEM(full, f32),
+            pltpu.VMEM(full, bf16),
+            pltpu.VMEM(full, f32),
+            pltpu.VMEM(full, f32),
+            pltpu.VMEM((length, FF - kept), f32),
+            pltpu.VMEM((length, kept + LANES), bf16),
+        ],
+        compiler_params=pltpu.CompilerParams(vmem_limit_bytes=60 * 2**20),
+        name="layer",
+    )(inputs, segment_row[None], cotangent, weights, gains.astype(f32).reshape(2, MODEL_WIDTH), freqs)
+
+
+def columns_to_panels(matrix):
+    return matrix.reshape(matrix.shape[0], -1, LANES).swapaxes(0, 1).reshape(-1, LANES)
+
+
+def panels_to_columns(panels, rows):
+    return panels.reshape(-1, rows, LANES).swapaxes(0, 1).reshape(rows, -1)
+
+
+def block_to_panels(flat, group):
+    inner = QUERY_HEADS * HEAD_SIZE
+    qkv = inner + 2 * KEY_VALUE_HEADS * HEAD_SIZE
+    cut = MODEL_WIDTH * qkv
+
+    def joint(v):
+        out, w = v[cut:].reshape(inner, MODEL_WIDTH), v[:cut].reshape(MODEL_WIDTH, qkv)
+        return columns_to_panels(jnp.concatenate([out, w], axis=1))
+
+    def gateup(v):
+        return columns_to_panels(v.reshape(-1, 2 * FF))
+
+    def down(v):
+        return columns_to_panels(v.reshape(FF, MODEL_WIDTH).T)
+
+    return lax.switch(group, [joint, gateup, gateup, down], flat)
+
+
+def panels_to_block(panels, group):
+    inner = QUERY_HEADS * HEAD_SIZE
+
+    def joint(v):
+        both = panels_to_columns(v, MODEL_WIDTH)
+        return jnp.concatenate([both[:, MODEL_WIDTH:].reshape(-1), both[:, :MODEL_WIDTH].reshape(-1)])
+
+    def gateup(v):
+        return panels_to_columns(v, MODEL_WIDTH // 2).reshape(-1)
+
+    def down(v):
+        return panels_to_columns(v, MODEL_WIDTH).T.reshape(-1)
+
+    return lax.switch(group, [joint, gateup, gateup, down], panels)
+
+
 def on_device(inputs, segments, cotangent, params, moment_one, moment_two):
     groups = lax.axis_size("group")
     wides = lax.axis_size("wide")
@@ -583,19 +857,41 @@
 
     rounded = params.astype(jnp.bfloat16)
     tail = jnp.pad(rounded[share_len - gain_len :], (0, 16 * LANES - gain_len)).reshape(16, LANES)
-    tails = gather_tails(tail, groups).reshape(groups, -1)[:, :gain_len]
+    tails = gather_tails(tail, groups, 0).reshape(groups, -1)[:, :gain_len]
     before = lax.dynamic_index_in_dim(tails, (group + groups - 1) % groups, keepdims=False)
     joined = jnp.concatenate([before, rounded])
     block = lax.dynamic_slice(joined, (gain_len - extra * group,), (block_len,))
-    gathered = gather_blocks(to_pieces(block)[0], groups, count, 2)
-    weights = unpack(from_pieces(gathered), tails[groups - 1])
-    outputs, d_inputs, main, gains = layer_row(inputs[0], segments[0], cotangent[0], weights)
+    by_panels = groups == 4 and block_len == MODEL_WIDTH * FF and not padding
+    flat_gains = tails[groups - 1]
+    if by_panels:
+        block = block_to_panels(block, group)
+        gathered = gather_blocks(to_pieces(block)[0], groups, count, 2)
+        outputs, d_inputs, main, gains = layer_panels(
+            inputs[0],
+            segments[0],
+            cotangent[0],
+            gathered.reshape(groups, block_rows, LANES),
+            flat_gains,
+        )
+        gains = gains.reshape(-1)
+    else:
+        gathered = gather_blocks(to_pieces(block)[0], groups, count, 2)
+        weights = unpack(from_pieces(gathered), flat_gains)
+        outputs, d_inputs, main, gains = layer_row(inputs[0], segments[0], cotangent[0], weights)
     gains = gains.astype(jnp.bfloat16).astype(jnp.float32)
     gains = jnp.pad(gains, (0, 16 * LANES - gain_len)).reshape(16, LANES)
     summed_block, head, gains, square = sum_blocks(to_pieces(main), gains, groups, count, chunks)
     gains = gains.reshape(-1)[:gain_len].astype(jnp.bfloat16)
-    head = jnp.where(group == groups - 1, gains, head.reshape(-1)[:gain_len])
-    joined = jnp.concatenate([from_pieces(summed_block).reshape(-1), head])
+    if by_panels:
+        flat_block = panels_to_block(from_pieces(summed_block), group)
+        head = jnp.pad(flat_block[:gain_len], (0, 16 * LANES - gain_len)).reshape(16, LANES)
+        heads = gather_tails(head, groups, 3).reshape(groups, -1)[:, :gain_len]
+        head = lax.dynamic_index_in_dim(heads, (group + 1) % groups, keepdims=False)
+    else:
+        flat_block = from_pieces(summed_block).reshape(-1)
+        head = head.reshape(-1)[:gain_len]
+    head = jnp.where(group == groups - 1, gains, head)
+    joined = jnp.concatenate([flat_block, head])
     summed = lax.dynamic_slice(joined, (extra * group,), (share_len,)).astype(jnp.float32)
     gains = gains.astype(jnp.float32)
     squares = jnp.sum(square) + jnp.sum(gains * gains)

time: 221 us -> 194 us (0.88)
  Pallas kernels: 121 us -> 142 us
  matrix products: 19.8 us -> 0 us
  other arithmetic: 37.8 us -> 23.1 us
  local copies, waits for them, and re-layouts: 38.3 us -> 26.7 us
    reshape x8 -> x3, local copies, waits for them, and re-layouts: 24.5 us -> 3.01 us  [the longest x1 1.26 us: joint(): both[:, MODEL_WIDTH:].reshape(-1)]
    dot_general x18 -> x0, matrix products: 19.8 us -> none  [the longest x4 5.01 us: inner_rows(): lax.dot_general(left_op, right_op, (((0,), (0,)), ((), ())), preferred_el...]
    pallas_call x0 -> x1, Pallas kernels: none -> 16.6 us  [layer_panels(): pl.pallas_call(layer_kernel, out_shape=(jax.ShapeDtypeStruct(full, bf16),...]
    concatenate x3 -> x2, other arithmetic: 12.3 us -> 3.16 us  [the longest x1 1.83 us: joint(): return columns_to_panels(jnp.concatenate([out, w], axis=1))]
    unnamed x89 -> x10, local copies, waits for them, and re-layouts: 1.07 us -> 8.28 us
    pallas_call x1 -> x2, Pallas kernels: 8.6 us -> 15.3 us  [gather_tails(): pl.pallas_call(functools.partial(tails_kernel, groups, 0), out_shape=jax....]
    another operation x0 -> x5, local copies, waits for them, and re-layouts: none -> 4.23 us  [the longest x1 2.26 us: panels_to_columns(): return panels.reshape(-1, rows, LANES).swapaxes(0, 1).reshape(rows, -1)]
    slice x8 -> x9, local copies, waits for them, and re-layouts: 8.51 us -> 4.7 us  [the longest x2 2.45 us: joint(): both[:, MODEL_WIDTH:].reshape(-1)]
where the time goes in v2:
time: 194 us
  Pallas kernels  142 us (73%)
  local copies, waits for them, and re-layouts  26.7 us (14%)
  other arithmetic  23.1 us (12%)
  between operations  2.11 us (1%)
    pallas_call x1, Pallas kernels, sum_blocks(): pl.pallas_call(functools.partial(sum_kernel, groups, count, chunks), out_...  66.7 us
    pallas_call x1, Pallas kernels, gather_blocks(): pl.pallas_call(functools.partial(gather_kernel, groups, count, chunks), o...  43.1 us
    pallas_call x1, Pallas kernels, layer_panels(): pl.pallas_call(layer_kernel, out_shape=(jax.ShapeDtypeStruct(full, bf16),...  16.6 us
    pallas_call x2, Pallas kernels, gather_tails(): pl.pallas_call(functools.partial(tails_kernel, groups, 0), out_shape=jax....  15.3 us
    sub x1, other arithmetic, adam_update(): new_params = params - learn_rate * (step_size + decay_term)  11.8 us
    unnamed x10, local copies, waits for them, and re-layouts  8.28 us

profile of v2, /device:TPU:0, one launch (start us, length us, event | category | flops | bytes accessed | tf_op | source)
XLA Modules:
  0.0 193.7 jit_solution(11970965207036587419)
XLA Ops:
  1.3 1.7 copy.40
  3.0 1.7 copy.41
  4.7 2.2 %convert_element_type.37 = bf16[885024]{0:T(1024)(128)(2,1)S(1)} convert(f32[885024]{0:T(1024)} %param.17) | non-fusion elementwise | flops 885024 | bytes 5310144 | tf_op jit(solution)/shard_map/convert_element_type | solution.py:858
  7.6 8.6 %tails.2 = bf16[4,16,128]{2,1,0:T(8,128)(2,1)} custom-call(bf16[16,128]{1,0:T(8,128)(2,1)} %pad_bitcast_fusion.tail_ref), custom_call_target="tpu_custom_call" | custom-call | tf_op jit(solution)/shard_map/tails/pallas_call | solution.py:488
  17.0 1.4 fusion.3
  19.1 8.5 %conditional.2 = (bf16[6912,128]{1,0:T(8,128)(2,1)}) conditional(s32[]{:T(128)} %clamp.4, bf16[884736]{0:T(1024)(128)(2,1)S(1)} %fusion.3, bf16[884736]{0:T(1024)(128)(2,1)S(1)} %fusion.3, bf16[884736]{0:T(1024)(128)(2,1)S(1)} %fusion.3, bf16[884736]{0:T(1024)(128)(2,1)S(1)} %fusion.3), branch_computations={%region_0.1_spmd, %region_1.2_spmd, %region_2.3_spmd, %region_3.4_... | conditional | flops 3538944 | bytes 17694728 | solution.py:813
  20.8 1.8 pad_maximum_fusion
  22.6 2.7 %copy.28 = bf16[576,1536]{0,1:T(8,128)(2,1)S(1)} copy(bf16[576,1536]{1,0:T(8,128)(2,1)} %pad_maximum_fusion) | data formatting | bytes 3538944 | tf_op jit(solution)/shard_map/cond/branch_0_fun/concatenate | solution.py:805
  25.4 2.2 %copy.29 = bf16[12,576,128]{2,1,0:T(8,128)(2,1)} copy(bf16[12,576,128]{1,2,0:T(8,128)(2,1)S(1)} %bitcast.71) | data formatting | bytes 3538944 | tf_op jit(solution)/shard_map/cond/branch_0_fun/transpose | solution.py:791
  27.6 43.1 %gather_weights.1 = bf16[4,2,2,2,864,128]{5,4,3,2,1,0:T(8,128)(2,1)} custom-call(bf16[2,2,2,864,128]{4,3,2,1,0:T(8,128)(2,1)} %bitcast.80), custom_call_target="tpu_custom_call" | custom-call | tf_op jit(solution)/shard_map/gather_weights/pallas_call | solution.py:502
  70.7 16.6 %layer.1 = (bf16[128,576]{1,0:T(8,128)(2,1)}, bf16[128,576]{1,0:T(8,128)(2,1)}, bf16[4,6912,128]{2,1,0:T(8,128)(2,1)}, f32[2,576]{1,0:T(2,128)}) custom-call(bf16[128,576]{1,0:T(8,128)(2,1)} %bitcast.81, s32[1,128]{1,0:T(1,128)} %seg_ref.1, bf16[128,576]{1,0:T(8,128)(2,1)} %bitcast.82, bf16[4,6912,128]{2,1,0:T(8,128)(2,1)} %bitcast.68, ...), custom_call_target="tpu_custom_call" | custom-call | tf_op jit(solution)/shard_map/layer/pallas_call | solution.py:766
  87.3 1.7 copy.42
  89.0 1.7 copy.43
  92.1 66.7 %sum_grads.1 = (bf16[2,2,2,864,128]{4,3,2,1,0:T(8,128)(2,1)S(1)}, bf16[16,128]{1,0:T(8,128)(2,1)}, f32[16,128]{1,0:T(8,128)}, f32[8,128]{1,0:T(8,128)}) custom-call(bf16[4,2,2,2,864,128]{5,4,3,2,1,0:T(8,128)(2,1)} %bitcast.75, f32[16,128]{1,0:T(8,128)} %bitcast_convert_fusion.gain_ref), custom_call_target="tpu_custom_call" | custom-call | tf_op jit(solution)/shard_map/sum_grads/pallas_call | solution.py:528
  158.8 1.3 multiply_reduce_fusion
  160.1 1.3 reduce_sum.18
  162.7 11.0 %conditional.3 = (bf16[884736]{0:T(1024)(128)(2,1)}, bf16[16,128]{1,0:T(8,128)(2,1)S(1)}) conditional(s32[]{:T(128)} %clamp.4, bf16[2,2,2,864,128]{4,3,2,1,0:T(8,128)(2,1)S(1)} %get-tuple-element.34, bf16[2,2,2,864,128]{4,3,2,1,0:T(8,128)(2,1)S(1)} %get-tuple-element.34, ...), branch_computations={%region_4.5_spmd, %region_5.6_spmd, %region_6.7_spmd, %region_7.8_... | conditional | flops 3538944 | bytes 19914768 | solution.py:829
  162.7 2.3 %copy.33 = bf16[12,576,128]{1,2,0:T(8,128)(2,1)} copy(bf16[12,576,128]{2,1,0:T(8,128)(2,1)S(1)} %bitcast.64) | data formatting | bytes 3538944 | tf_op jit(solution)/shard_map/cond/branch_0_fun/reshape;reshape;reshape | solution.py:795
  166.2 1.4 slice.65
  169.8 1.4 reshape.117
  171.2 1.3 reshape.115
  172.4 1.3 pad_maximum_fusion.1
  174.4 6.7 %tails.3 = bf16[4,16,128]{2,1,0:T(8,128)(2,1)} custom-call(bf16[16,128]{1,0:T(8,128)(2,1)} %broadcast_select_fusion.tail_ref), custom_call_target="tpu_custom_call" | custom-call | tf_op jit(solution)/shard_map/tails/pallas_call | solution.py:488
  181.9 11.8 %multiply_subtract_fusion = (f32[885024]{0:T(1024)}, f32[885024]{0:T(1024)}, f32[885024]{0:T(1024)}, f32[885024]{0:T(1024)}) fusion(f32[885024]{0:T(1024)} %param.17, s32[]{:T(128)S(6)} %mul.65, f32[]{:T(128)S(6)} %min.3, f32[885024]{0:T(1024)} %param.18, f32[885024]{0:T(1024)} %param.19, s32[]{:T(128)S(6)} %select_n.43, ...), kind=kLoop, calls=%fused_computation.4 | loop fusion | flops 20355552 | bytes 26552460 | tf_op jit(solution)/shard_map/sub | solution.py:224
  (31 shorter events, 10.6 us)
Async XLA Ops:
  162.7 11.1 %copy-start.2 = (pred[16,128]{1,0:T(8,128)(4,1)S(1)}, pred[16,128]{1,0:T(8,128)(4,1)}, u32[]{:S(2)}) copy-start(pred[16,128]{1,0:T(8,128)(4,1)} %constant.68.clone.1) | copy-start | bytes 6148
  162.7 19.2 %copy-start.1 = (f32[16,128]{1,0:T(8,128)S(1)}, f32[16,128]{1,0:T(8,128)}, u32[]{:S(2)}) copy-start(f32[16,128]{1,0:T(8,128)} %get-tuple-element.36) | copy-start | bytes 24580

commit v3 on v2

--- a/solution.py
+++ b/solution.py
@@ -289,35 +289,95 @@
         index = [slice(None) if b in open_bits else bits[b] for b in reversed(range(count))]
         return ref.at[tuple(lead + index + [pl.ds(chunk * step, step)])]
 
+    def copy(src, dst, send_sem, recv_sem, peer):
+        return pltpu.make_async_remote_copy(
+            src_ref=src,
+            dst_ref=dst,
+            send_sem=send_sem,
+            recv_sem=recv_sem,
+            device_id=peer,
+            device_id_type=MESH,
+        )
+
+    def along(way, d, c):
+        source = (group - way * (d - 1) + groups) % groups
+        unit = (0 if way > 0 else groups - 1) + d - 1
+        src = place(block_ref, [], [], c) if d == 1 else place(out_ref, [source], [], c)
+        return copy(
+            src,
+            place(out_ref, [source], [], c),
+            zs.at[unit, c],
+            zr.at[unit, c],
+            (wide, (group + way + groups) % groups),
+        )
+
+    def passes(way, d):
+        ahead = group + way
+        behind = group - way * (d - 1)
+        return (ahead >= 0) & (ahead < groups) & (behind >= 0) & (behind < groups)
+
+    def comes(way, d):
+        behind = group - way * d
+        return (behind >= 0) & (behind < groups)
+
+    def across(way, d, c, stage):
+        order = bit_order(c, count)[::-1]
+        b = order[stage]
+        source = (group - way * d + groups) % groups
+        unit = (0 if way > 0 else groups - 1) + d - 1
+        here = place(out_ref, [source], order[:stage], c)
+        return copy(
+            here,
+            here,
+            ws.at[unit, c, stage],
+            wr.at[unit, c, stage],
+            (flipped(wide, bits[b], b), group),
+        )
+
     units = [(d, c) for d in range(1, groups) for c in range(chunks)]
-    copies = {}
-    for u, (d, c) in enumerate(units):
-        copies[u, 0] = send(
-            place(block_ref, [], [], c),
-            place(out_ref, [group], [], c),
-            zs.at[u],
-            zr.at[u],
-            (wide, (group + d) % groups),
-        )
+    for c in range(chunks):
+        for way in (1, -1):
+
+            @pl.when(passes(way, 1))
+            def _():
+                along(way, 1, c).start()
+
     own = pltpu.make_async_copy(block_ref, out_ref.at[group], own_sem)
     own.start()
-    for tick in range(len(units) // chunks + count + 1):
-        for u, (d, c) in enumerate(units):
-            stage = tick - u // chunks
+    for tick in range(len(units) // 2 + count + 1):
+        for u, (d, c) in reversed(list(enumerate(units))):
+            stage = tick - u // 2
             if not 0 <= stage <= count:
                 continue
-            copies[u, stage].wait_recv()
-            if stage == count:
-                continue
-            order = bit_order(c, count)[::-1]
-            b = order[stage]
-            source = (group + groups - d) % groups
-            here = place(out_ref, [source], order[:stage], c)
-            copies[u, stage + 1] = send(
-                here, here, ws.at[u, stage], wr.at[u, stage], (flipped(wide, bits[b], b), group)
-            )
-    for copy in copies.values():
-        copy.wait_send()
+            for way in (1, -1):
+
+                @pl.when(comes(way, d))
+                def _():
+                    if stage == 0:
+                        along(way, d, c).wait_recv()
+                    else:
+                        across(way, d, c, stage - 1).wait_recv()
+                    if stage < count:
+                        across(way, d, c, stage).start()
+
+                if stage == 0 and d + 1 < groups:
+
+                    @pl.when(passes(way, d + 1))
+                    def _():
+                        along(way, d + 1, c).start()
+
+    for way in (1, -1):
+        for d, c in units:
+
+            @pl.when(passes(way, d))
+            def _():
+                along(way, d, c).wait_send()
+
+            @pl.when(comes(way, d))
+            def _():
+                for stage in range(count):
+                    across(way, d, c, stage).wait_send()
+
     own.wait()
 
 
@@ -461,13 +521,17 @@
     gains = gain_z[0]
     for d in range(1, groups):
         gains = gains + gain_z[d]
+    gains = gains.astype(jnp.bfloat16).astype(f32)
     gsum_ref[...] = gains
     for d in range(1, groups):
         copies["q", d].wait_recv()
     square = sq_z[0]
     for d in range(1, groups):
         square = square + sq_z[d]
-    sq_ref[...] = square
+    square = square + jnp.sum((gains * gains).reshape(-1, 8, LANES), axis=0)
+    total = jnp.sum(jnp.sum(square, axis=-1, keepdims=True), axis=0, keepdims=True)
+    clip = jnp.minimum(jnp.float32(1.0), max_norm * lax.rsqrt(total))
+    sq_ref[...] = jnp.broadcast_to(clip, sq_ref.shape)
     copies["h"].wait_recv()
     for copy in copies.values():
         copy.wait_send()
@@ -498,7 +562,7 @@
 
 def gather_blocks(block, groups, count, chunks):
     dma = pltpu.SemaphoreType.DMA
-    units = (groups - 1) * chunks
+    units = 2 * (groups - 1)
     return pl.pallas_call(
         functools.partial(gather_kernel, groups, count, chunks),
         out_shape=jax.ShapeDtypeStruct((groups,) + block.shape, block.dtype),
@@ -506,10 +570,10 @@
         out_specs=vmem_specs(1)[0],
         scratch_shapes=[
             dma,
-            dma((units,)),
-            dma((units,)),
-            dma((units, count)),
-            dma((units, count)),
+            dma((units, chunks)),
+            dma((units, chunks)),
+            dma((units, chunks, count)),
+            dma((units, chunks, count)),
         ],
         compiler_params=params_of(1),
         name="gather_weights",
@@ -567,10 +631,10 @@
 def layer_kernel(
     x_ref, seg_ref, cot_ref, w_ref, gain_ref, freq_ref,
     out_ref, din_ref, main_ref, gg_ref,
-    att_s, mid_s, hid_s, down_s, dhid_s, dproj_s, dmid_s,
+    att_s, mid_s, hid_s, down_s, dhid_s, dproj_s, dmid_s, cot_s,
 ):
     f32, bf16 = jnp.float32, jnp.bfloat16
-    width, length, half = MODEL_WIDTH, x_ref.shape[0], HEAD_SIZE // 2
+    width, length, half = MODEL_WIDTH, x_ref.shape[1], HEAD_SIZE // 2
     part = width // 2
     heads, kv = QUERY_HEADS, KEY_VALUE_HEADS
     repeat = heads // kv
@@ -584,7 +648,8 @@
         return jnp.concatenate([zero_panel(p), zero_panel(p + 1)], axis=-1)
 
     gain_one, gain_two = gain_ref[0:1, :], gain_ref[1:2, :]
-    x = x_ref[...].astype(f32)
+    x = x_ref[...].astype(f32).T
+    cot_s[...] = cot_ref[...].astype(f32).T.astype(bf16)
     inv_attn = lax.rsqrt(jnp.mean(x * x, axis=-1, keepdims=True) + norm_eps)
     normed_attn = x * inv_attn
     hidden_attn = (normed_attn * gain_one).astype(bf16)
@@ -665,7 +730,7 @@
 
     def hidden_step(i, _):
         p = 2 * i
-        hidden, cotangent = hid_s[...], cot_ref[...]
+        hidden, cotangent = hid_s[...], cot_s[...]
         gate_w, up_w = gateup_pair(p), gateup_pair(p + half_panels)
         down_rows = [pl.ds(pl.multiple_of((p + q) * width, width), width) for q in range(2)]
         down_w = jnp.concatenate([w_ref[3, r, :] for r in down_rows], axis=-1)
@@ -679,7 +744,7 @@
         dhid_s[...] += dot(d_gate, gate_w, 1, 1) + dot(d_upper, up_w, 1, 1)
         store_gateup(p, dot(hidden, d_gate, 0, 0))
         store_gateup(p + half_panels, dot(hidden, d_upper, 0, 0))
-        d_down = dot(cotangent, activation, 0, 0).astype(bf16)
+        d_down = dot(cot_ref[...], activation, 1, 0).astype(bf16)
         for q in range(2):
             main_ref[3, down_rows[q], :] = d_down[:, q * LANES : (q + 1) * LANES]
         return 0
@@ -687,10 +752,10 @@
     lax.fori_loop(0, half_panels // 2, hidden_step, 0)
     mid = mid_s[...]
     normed_ffn = mid * inv_ffn
-    out_ref[...] = (mid + down_s[...]).astype(bf16)
+    out_ref[...] = (mid + down_s[...]).T.astype(bf16)
     d_hidden = dhid_s[...]
     gg_ref[1:2, :] = jnp.sum(d_hidden * normed_ffn, axis=0, keepdims=True)
-    d_mid = cot_ref[...].astype(f32) + norm_back(d_hidden, normed_ffn, inv_ffn, gain_two)
+    d_mid = cot_s[...].astype(f32) + norm_back(d_hidden, normed_ffn, inv_ffn, gain_two)
     dmid_s[...] = jnp.zeros_like(dmid_s)
     dmid_s[:, :width] = d_mid.astype(bf16)
     attended = att_s[...]
@@ -752,7 +817,7 @@
         main_ref[0, pl.ds(p * width, width), :] = left.astype(bf16)
         main_ref[0, pl.ds((p + 1) * width, width), :] = value[:, LANES:].astype(bf16)
     gg_ref[0:1, :] = jnp.sum(d_hidden * normed_attn, axis=0, keepdims=True)
-    din_ref[...] = (d_mid + norm_back(d_hidden, normed_attn, inv_attn, gain_one)).astype(bf16)
+    din_ref[...] = (d_mid + norm_back(d_hidden, normed_attn, inv_attn, gain_one)).T.astype(bf16)
 
 
 def layer_panels(inputs, segment_row, cotangent, weights, gains):
@@ -763,11 +828,11 @@
     freqs = jnp.tile(freqs, LANES // half)[None]
     full = (length, MODEL_WIDTH)
     kept = (QUERY_HEADS * HEAD_SIZE) // LANES * LANES
-    return pl.pallas_call(
+    outputs, d_inputs, main, gains = pl.pallas_call(
         layer_kernel,
         out_shape=(
-            jax.ShapeDtypeStruct(full, bf16),
-            jax.ShapeDtypeStruct(full, bf16),
+            jax.ShapeDtypeStruct(full[::-1], bf16),
+            jax.ShapeDtypeStruct(full[::-1], bf16),
             jax.ShapeDtypeStruct(weights.shape, bf16),
             jax.ShapeDtypeStruct((2, MODEL_WIDTH), f32),
         ),
@@ -781,10 +846,12 @@
             pltpu.VMEM(full, f32),
             pltpu.VMEM((length, FF - kept), f32),
             pltpu.VMEM((length, kept + LANES), bf16),
+            pltpu.VMEM(full, bf16),
         ],
         compiler_params=pltpu.CompilerParams(vmem_limit_bytes=60 * 2**20),
         name="layer",
-    )(inputs, segment_row[None], cotangent, weights, gains.astype(f32).reshape(2, MODEL_WIDTH), freqs)
+    )(inputs.T, segment_row[None], cotangent.T, weights, gains.astype(f32).reshape(2, MODEL_WIDTH), freqs)
+    return (outputs.T, d_inputs.T, main, gains)
 
 
 def columns_to_panels(matrix):
@@ -844,6 +911,9 @@
     piece_rows = -(-piece_rows // (16 * chunks)) * 16 * chunks
     padding = piece_rows * wides - block_rows
     lead = (2,) * count
+    slices = chunks
+    if piece_rows % 288 == 0:
+        chunks = 18
 
     def to_pieces(rows):
         rows = rows.reshape(-1, block_rows, LANES)
@@ -865,7 +935,7 @@
     flat_gains = tails[groups - 1]
     if by_panels:
         block = block_to_panels(block, group)
-        gathered = gather_blocks(to_pieces(block)[0], groups, count, 2)
+        gathered = gather_blocks(to_pieces(block)[0], groups, count, slices)
         outputs, d_inputs, main, gains = layer_panels(
             inputs[0],
             segments[0],
@@ -875,7 +945,7 @@
         )
         gains = gains.reshape(-1)
     else:
-        gathered = gather_blocks(to_pieces(block)[0], groups, count, 2)
+        gathered = gather_blocks(to_pieces(block)[0], groups, count, slices)
         weights = unpack(from_pieces(gathered), flat_gains)
         outputs, d_inputs, main, gains = layer_row(inputs[0], segments[0], cotangent[0], weights)
     gains = gains.astype(jnp.bfloat16).astype(jnp.float32)
@@ -893,9 +963,7 @@
     head = jnp.where(group == groups - 1, gains, head)
     joined = jnp.concatenate([flat_block, head])
     summed = lax.dynamic_slice(joined, (extra * group,), (share_len,)).astype(jnp.float32)
-    gains = gains.astype(jnp.float32)
-    squares = jnp.sum(square) + jnp.sum(gains * gains)
-    clip_factor = jnp.minimum(jnp.float32(1.0), max_norm * lax.rsqrt(squares))
+    clip_factor = square[0, 0]
     flat_index = group * share_len + jnp.arange(share_len, dtype=jnp.int32)
     decay_mask = flat_index < share_len * groups - gain_len
     new_params, new_moment_one, new_moment_two = adam_update(

time: 194 us -> 191 us (0.985)
  local copies, waits for them, and re-layouts: 26.7 us -> 21.1 us
  Pallas kernels: 142 us -> 147 us
  other arithmetic: 23.1 us -> 21.1 us
    unnamed x10 -> x6, local copies, waits for them, and re-layouts: 8.28 us -> 1.46 us
    pallas_call x1, Pallas kernels: 66.7 us -> 73.4 us  [sum_blocks(): pl.pallas_call(functools.partial(sum_kernel, groups, count, chunks), out_...]
    reduce_sum x2 -> x0, other arithmetic: 2.58 us -> none  [on_device(): squares = jnp.sum(square) + jnp.sum(gains * gains)]
where the time goes in v3:
time: 191 us; the launch traced here: 190 us
  Pallas kernels  147 us (77%)
  other arithmetic  21.1 us (11%)
  local copies, waits for them, and re-layouts  21.1 us (11%)
    pallas_call x1, Pallas kernels, sum_blocks(): pl.pallas_call(functools.partial(sum_kernel, groups, count, chunks), out_...  73.4 us
    pallas_call x1, Pallas kernels, gather_blocks(): pl.pallas_call(functools.partial(gather_kernel, groups, count, chunks), o...  41.6 us
    pallas_call x1, Pallas kernels, layer_panels(): pl.pallas_call(layer_kernel, out_shape=(jax.ShapeDtypeStruct(full[::-1],...  16.7 us
    pallas_call x2, Pallas kernels, gather_tails(): pl.pallas_call(functools.partial(tails_kernel, groups, 0), out_shape=jax....  15.3 us
    sub x1, other arithmetic, adam_update(): new_params = params - learn_rate * (step_size + decay_term)  12.4 us

profile of v3, /device:TPU:0, one launch (start us, length us, event | category | flops | bytes accessed | tf_op | source)
XLA Modules:
  0.0 190.2 jit_solution(18380402948364044341)
XLA Ops:
  1.3 2.2 %convert_element_type.30 = bf16[885024]{0:T(1024)(128)(2,1)S(1)} convert(f32[885024]{0:T(1024)} %param.17) | non-fusion elementwise | flops 885024 | bytes 5310144 | tf_op jit(solution)/shard_map/convert_element_type | solution.py:928
  4.2 8.6 %tails.2 = bf16[4,16,128]{2,1,0:T(8,128)(2,1)} custom-call(bf16[16,128]{1,0:T(8,128)(2,1)} %pad_bitcast_fusion.tail_ref), custom_call_target="tpu_custom_call" | custom-call | tf_op jit(solution)/shard_map/tails/pallas_call | solution.py:552
  12.8 0.7 copy.37
  13.6 1.4 fusion.3
  15.7 8.5 %conditional.2 = (bf16[6912,128]{1,0:T(8,128)(2,1)}) conditional(s32[]{:T(128)} %clamp.4, bf16[884736]{0:T(1024)(128)(2,1)S(1)} %fusion.3, bf16[884736]{0:T(1024)(128)(2,1)S(1)} %fusion.3, bf16[884736]{0:T(1024)(128)(2,1)S(1)} %fusion.3, bf16[884736]{0:T(1024)(128)(2,1)S(1)} %fusion.3), branch_computations={%region_0.1_spmd, %region_1.2_spmd, %region_2.3_spmd, %region_3.4_... | conditional | flops 3538944 | bytes 17694728 | solution.py:880
  15.8 1.0 reshape.104
  17.4 1.8 pad_maximum_fusion
  19.2 2.7 %copy.20 = bf16[576,1536]{0,1:T(8,128)(2,1)S(1)} copy(bf16[576,1536]{1,0:T(8,128)(2,1)} %pad_maximum_fusion) | data formatting | bytes 3538944 | tf_op jit(solution)/shard_map/cond/branch_0_fun/concatenate | solution.py:872
  22.0 2.2 %copy.21 = bf16[12,576,128]{2,1,0:T(8,128)(2,1)} copy(bf16[12,576,128]{1,2,0:T(8,128)(2,1)S(1)} %bitcast.82) | data formatting | bytes 3538944 | tf_op jit(solution)/shard_map/cond/branch_0_fun/transpose | solution.py:858
  24.2 41.6 %gather_weights.1 = bf16[4,2,2,2,864,128]{5,4,3,2,1,0:T(8,128)(2,1)} custom-call(bf16[2,2,2,864,128]{4,3,2,1,0:T(8,128)(2,1)} %bitcast.91), custom_call_target="tpu_custom_call" | custom-call | tf_op jit(solution)/shard_map/gather_weights/pallas_call | solution.py:566
  65.9 16.7 %layer.1 = (bf16[576,128]{1,0:T(8,128)(2,1)}, bf16[576,128]{1,0:T(8,128)(2,1)}, bf16[4,6912,128]{2,1,0:T(8,128)(2,1)}, f32[2,576]{1,0:T(2,128)}) custom-call(bf16[576,128]{1,0:T(8,128)(2,1)} %bitcast.92, s32[1,128]{1,0:T(1,128)} %seg_ref.1, bf16[576,128]{1,0:T(8,128)(2,1)} %bitcast.93, bf16[4,6912,128]{2,1,0:T(8,128)(2,1)} %bitcast.79, ...), custom_call_target="tpu_custom_call" | custom-call | tf_op jit(solution)/shard_map/layer/pallas_call | solution.py:831
  84.0 73.4 %sum_grads.1 = (bf16[2,2,2,864,128]{4,3,2,1,0:T(8,128)(2,1)S(1)}, bf16[16,128]{1,0:T(8,128)(2,1)}, f32[16,128]{1,0:T(8,128)}, f32[8,128]{1,0:T(8,128)}) custom-call(bf16[4,2,2,2,864,128]{5,4,3,2,1,0:T(8,128)(2,1)} %bitcast.86, f32[16,128]{1,0:T(8,128)} %bitcast_convert_fusion.gain_ref), custom_call_target="tpu_custom_call" | custom-call | tf_op jit(solution)/shard_map/sum_grads/pallas_call | solution.py:592
  157.4 1.2 slice.69
  158.6 11.0 %conditional.3 = (bf16[884736]{0:T(1024)(128)(2,1)}, bf16[16,128]{1,0:T(8,128)(2,1)S(1)}) conditional(s32[]{:T(128)} %clamp.4, bf16[2,2,2,864,128]{4,3,2,1,0:T(8,128)(2,1)S(1)} %get-tuple-element.34, bf16[2,2,2,864,128]{4,3,2,1,0:T(8,128)(2,1)S(1)} %get-tuple-element.34, ...), branch_computations={%region_4.5_spmd, %region_5.6_spmd, %region_6.7_spmd, %region_7.8_... | conditional | flops 3538944 | bytes 19914768 | solution.py:896
  158.6 2.2 %copy.25 = bf16[12,576,128]{1,2,0:T(8,128)(2,1)} copy(bf16[12,576,128]{2,1,0:T(8,128)(2,1)S(1)} %bitcast.75) | data formatting | bytes 3538944 | tf_op jit(solution)/shard_map/cond/branch_0_fun/reshape;reshape;reshape | solution.py:862
  160.9 1.2 slice.71
  162.0 1.4 slice.70
  163.4 1.1 copy.26
  164.9 0.8 reshape.116
  165.6 1.4 reshape.117
  167.0 1.3 reshape.115
  168.3 1.3 pad_maximum_fusion.1
  170.2 6.7 %tails.3 = bf16[4,16,128]{2,1,0:T(8,128)(2,1)} custom-call(bf16[16,128]{1,0:T(8,128)(2,1)} %broadcast_select_fusion.tail_ref), custom_call_target="tpu_custom_call" | custom-call | tf_op jit(solution)/shard_map/tails/pallas_call | solution.py:552
  177.8 12.4 %multiply_subtract_fusion = (f32[885024]{0:T(1024)}, f32[885024]{0:T(1024)}, f32[885024]{0:T(1024)}, f32[885024]{0:T(1024)}) fusion(f32[885024]{0:T(1024)} %param.17, s32[]{:T(128)S(6)} %mul.60, f32[]{:T(128)} %bitcast.54, f32[885024]{0:T(1024)} %param.18, f32[885024]{0:T(1024)} %param.19, s32[]{:T(128)S(6)} %select_n.43, bf16[1152]{0:T(1024)(128)(2,1)S(1)} %fusion.6, ...), kind=kLoop, calls=%fused_computation.4 | loop fusion | flops 20355552 | bytes 26552460 | tf_op jit(solution)/shard_map/sub | solution.py:224
  (26 shorter events, 5.9 us)
Async XLA Ops:
  158.6 11.0 %copy-start.2 = (pred[16,128]{1,0:T(8,128)(4,1)S(1)}, pred[16,128]{1,0:T(8,128)(4,1)}, u32[]{:S(2)}) copy-start(pred[16,128]{1,0:T(8,128)(4,1)} %constant.66.clone.1) | copy-start | bytes 6148
  158.6 19.1 %copy-start.1 = (f32[16,128]{1,0:T(8,128)S(1)}, f32[16,128]{1,0:T(8,128)}, u32[]{:S(2)}) copy-start(f32[16,128]{1,0:T(8,128)} %get-tuple-element.36) | copy-start | bytes 24580

commit v4 on v3

--- a/solution.py
+++ b/solution.py
@@ -462,7 +462,7 @@
     copies["x", 0] = send(gain_w.at[0], gain_w.at[count + 1], xs.at[0], xr.at[0], partner(0))
 
     for tick in range(chunks // 2 + 2 * count + 1):
-        for c in range(chunks):
+        for c in reversed(range(chunks)):
             s = tick - c // 2
             if 0 <= s < count:
                 add_scatter(c, s)
@@ -911,9 +911,6 @@
     piece_rows = -(-piece_rows // (16 * chunks)) * 16 * chunks
     padding = piece_rows * wides - block_rows
     lead = (2,) * count
-    slices = chunks
-    if piece_rows % 288 == 0:
-        chunks = 18
 
     def to_pieces(rows):
         rows = rows.reshape(-1, block_rows, LANES)
@@ -935,7 +932,7 @@
     flat_gains = tails[groups - 1]
     if by_panels:
         block = block_to_panels(block, group)
-        gathered = gather_blocks(to_pieces(block)[0], groups, count, slices)
+        gathered = gather_blocks(to_pieces(block)[0], groups, count, chunks)
         outputs, d_inputs, main, gains = layer_panels(
             inputs[0],
             segments[0],
@@ -945,7 +942,7 @@
         )
         gains = gains.reshape(-1)
     else:
-        gathered = gather_blocks(to_pieces(block)[0], groups, count, slices)
+        gathered = gather_blocks(to_pieces(block)[0], groups, count, chunks)
         weights = unpack(from_pieces(gathered), flat_gains)
         outputs, d_inputs, main, gains = layer_row(inputs[0], segments[0], cotangent[0], weights)
     gains = gains.astype(jnp.bfloat16).astype(jnp.float32)

time: 191 us -> 179 us (0.937)
  Pallas kernels: 147 us -> 135 us
    pallas_call x1, Pallas kernels: 73.4 us -> 61.2 us  [sum_blocks(): pl.pallas_call(functools.partial(sum_kernel, groups, count, chunks), out_...]
where the time goes in v4:
time: 179 us; the launch traced here: 178 us
  Pallas kernels  135 us (75%)
  other arithmetic  21.1 us (12%)
  local copies, waits for them, and re-layouts  21.1 us (12%)
    pallas_call x1, Pallas kernels, sum_blocks(): pl.pallas_call(functools.partial(sum_kernel, groups, count, chunks), out_...  61.2 us
    pallas_call x1, Pallas kernels, gather_blocks(): pl.pallas_call(functools.partial(gather_kernel, groups, count, chunks), o...  41.6 us
    pallas_call x1, Pallas kernels, layer_panels(): pl.pallas_call(layer_kernel, out_shape=(jax.ShapeDtypeStruct(full[::-1],...  16.7 us
    pallas_call x2, Pallas kernels, gather_tails(): pl.pallas_call(functools.partial(tails_kernel, groups, 0), out_shape=jax....  15.3 us
    sub x1, other arithmetic, adam_update(): new_params = params - learn_rate * (step_size + decay_term)  12.4 us

profile of v4, /device:TPU:0, one launch (start us, length us, event | category | flops | bytes accessed | tf_op | source)
XLA Modules:
  0.0 178.0 jit_solution(18407634461931088049)
XLA Ops:
  1.3 2.2 %convert_element_type.30 = bf16[885024]{0:T(1024)(128)(2,1)S(1)} convert(f32[885024]{0:T(1024)} %param.17) | non-fusion elementwise | flops 885024 | bytes 5310144 | tf_op jit(solution)/shard_map/convert_element_type | solution.py:925
  4.2 8.6 %tails.2 = bf16[4,16,128]{2,1,0:T(8,128)(2,1)} custom-call(bf16[16,128]{1,0:T(8,128)(2,1)} %pad_bitcast_fusion.tail_ref), custom_call_target="tpu_custom_call" | custom-call | tf_op jit(solution)/shard_map/tails/pallas_call | solution.py:552
  12.8 0.7 copy.37
  13.6 1.4 fusion.3
  15.7 8.5 %conditional.2 = (bf16[6912,128]{1,0:T(8,128)(2,1)}) conditional(s32[]{:T(128)} %clamp.4, bf16[884736]{0:T(1024)(128)(2,1)S(1)} %fusion.3, bf16[884736]{0:T(1024)(128)(2,1)S(1)} %fusion.3, bf16[884736]{0:T(1024)(128)(2,1)S(1)} %fusion.3, bf16[884736]{0:T(1024)(128)(2,1)S(1)} %fusion.3), branch_computations={%region_0.1_spmd, %region_1.2_spmd, %region_2.3_spmd, %region_3.4_... | conditional | flops 3538944 | bytes 17694728 | solution.py:880
  15.8 1.0 reshape.104
  17.4 1.8 %pad_maximum_fusion = bf16[576,1536]{1,0:T(8,128)(2,1)} fusion(bf16[576,960]{1,0:T(8,128)(2,1)S(1)} %reshape.104, bf16[576,576]{1,0:T(8,128)(2,1)S(1)} %slice.50), kind=kLoop, calls=%fused_computation | loop fusion | flops 3538944 | bytes 3538944 | tf_op jit(solution)/shard_map/cond/branch_0_fun/concatenate | solution.py:872
  19.2 2.7 %copy.20 = bf16[576,1536]{0,1:T(8,128)(2,1)S(1)} copy(bf16[576,1536]{1,0:T(8,128)(2,1)} %pad_maximum_fusion) | data formatting | bytes 3538944 | tf_op jit(solution)/shard_map/cond/branch_0_fun/concatenate | solution.py:872
  22.0 2.2 %copy.21 = bf16[12,576,128]{2,1,0:T(8,128)(2,1)} copy(bf16[12,576,128]{1,2,0:T(8,128)(2,1)S(1)} %bitcast.82) | data formatting | bytes 3538944 | tf_op jit(solution)/shard_map/cond/branch_0_fun/transpose | solution.py:858
  24.2 41.6 %gather_weights.1 = bf16[4,2,2,2,864,128]{5,4,3,2,1,0:T(8,128)(2,1)} custom-call(bf16[2,2,2,864,128]{4,3,2,1,0:T(8,128)(2,1)} %bitcast.91), custom_call_target="tpu_custom_call" | custom-call | tf_op jit(solution)/shard_map/gather_weights/pallas_call | solution.py:566
  65.9 16.7 %layer.1 = (bf16[576,128]{1,0:T(8,128)(2,1)}, bf16[576,128]{1,0:T(8,128)(2,1)}, bf16[4,6912,128]{2,1,0:T(8,128)(2,1)}, f32[2,576]{1,0:T(2,128)}) custom-call(bf16[576,128]{1,0:T(8,128)(2,1)} %bitcast.92, s32[1,128]{1,0:T(1,128)} %seg_ref.1, bf16[576,128]{1,0:T(8,128)(2,1)} %bitcast.93, bf16[4,6912,128]{2,1,0:T(8,128)(2,1)} %bitcast.79, ...), custom_call_target="tpu_custom_call" | custom-call | tf_op jit(solution)/shard_map/layer/pallas_call | solution.py:831
  84.0 61.2 %sum_grads.1 = (bf16[2,2,2,864,128]{4,3,2,1,0:T(8,128)(2,1)S(1)}, bf16[16,128]{1,0:T(8,128)(2,1)}, f32[16,128]{1,0:T(8,128)}, f32[8,128]{1,0:T(8,128)}) custom-call(bf16[4,2,2,2,864,128]{5,4,3,2,1,0:T(8,128)(2,1)} %bitcast.86, f32[16,128]{1,0:T(8,128)} %bitcast_convert_fusion.gain_ref), custom_call_target="tpu_custom_call" | custom-call | tf_op jit(solution)/shard_map/sum_grads/pallas_call | solution.py:592
  145.2 1.2 slice.69
  146.4 11.0 %conditional.3 = (bf16[884736]{0:T(1024)(128)(2,1)}, bf16[16,128]{1,0:T(8,128)(2,1)S(1)}) conditional(s32[]{:T(128)} %clamp.4, bf16[2,2,2,864,128]{4,3,2,1,0:T(8,128)(2,1)S(1)} %get-tuple-element.34, bf16[2,2,2,864,128]{4,3,2,1,0:T(8,128)(2,1)S(1)} %get-tuple-element.34, ...), branch_computations={%region_4.5_spmd, %region_5.6_spmd, %region_6.7_spmd, %region_7.8_... | conditional | flops 3538944 | bytes 19914768 | solution.py:896
  146.4 2.2 %copy.25 = bf16[12,576,128]{1,2,0:T(8,128)(2,1)} copy(bf16[12,576,128]{2,1,0:T(8,128)(2,1)S(1)} %bitcast.75) | data formatting | bytes 3538944 | tf_op jit(solution)/shard_map/cond/branch_0_fun/reshape;reshape;reshape | solution.py:862
  148.7 1.2 slice.71
  149.8 1.4 slice.70
  151.2 1.1 copy.26
  152.7 0.8 reshape.116
  153.4 1.4 reshape.117
  154.8 1.3 reshape.115
  156.1 1.3 pad_maximum_fusion.1
  158.0 6.7 %tails.3 = bf16[4,16,128]{2,1,0:T(8,128)(2,1)} custom-call(bf16[16,128]{1,0:T(8,128)(2,1)} %broadcast_select_fusion.tail_ref), custom_call_target="tpu_custom_call" | custom-call | tf_op jit(solution)/shard_map/tails/pallas_call | solution.py:552
  165.6 12.4 %multiply_subtract_fusion = (f32[885024]{0:T(1024)}, f32[885024]{0:T(1024)}, f32[885024]{0:T(1024)}, f32[885024]{0:T(1024)}) fusion(f32[885024]{0:T(1024)} %param.17, s32[]{:T(128)S(6)} %mul.60, f32[]{:T(128)} %bitcast.54, f32[885024]{0:T(1024)} %param.18, f32[885024]{0:T(1024)} %param.19, s32[]{:T(128)S(6)} %select_n.43, bf16[1152]{0:T(1024)(128)(2,1)S(1)} %fusion.6, ...), kind=kLoop, calls=%fused_computation.4 | loop fusion | flops 20355552 | bytes 26552460 | tf_op jit(solution)/shard_map/sub | solution.py:224
  (26 shorter events, 5.9 us)
Async XLA Ops:
  146.4 11.0 %copy-start.2 = (pred[16,128]{1,0:T(8,128)(4,1)S(1)}, pred[16,128]{1,0:T(8,128)(4,1)}, u32[]{:S(2)}) copy-start(pred[16,128]{1,0:T(8,128)(4,1)} %constant.66.clone.1) | copy-start | bytes 6148
  146.4 19.1 %copy-start.1 = (f32[16,128]{1,0:T(8,128)S(1)}, f32[16,128]{1,0:T(8,128)}, u32[]{:S(2)}) copy-start(f32[16,128]{1,0:T(8,128)} %get-tuple-element.36) | copy-start | bytes 24580
